TPU v7x, 32 devices: a whole 2x2x4 slice. The times are simulated.
32 devices in a mesh: replica: 4 (over y, core), fsdp: 2 (over x), tensor: 4 (over z).
Axes of the slice: x: 2, y: 2, z: 4, core: 2. Of those that a mesh axis runs over, the one named last changes fastest.
Arguments:
- hidden: bfloat16 [1024, 8192], P(('replica', 'fsdp')), may hold values from -6 to 6
- key_weight: bfloat16 [4, 8192, 1024], P('replica', 'fsdp', 'tensor'), may hold values from -0.0625 to 0.0625
- key_grad: bfloat16 [1024, 1024], P(('replica', 'fsdp'), 'tensor'), may hold values from -6 to 6
- pseudo_grads: float32 [4, 64, 1024], P('replica', 'fsdp', 'tensor'), may hold values from -6 to 6
- outer_params: float32 [40, 64, 1024], P(None, ('fsdp', 'replica'), 'tensor'), may hold values from -6 to 6
- outer_moment: float32 [40, 64, 1024], P(None, ('fsdp', 'replica'), 'tensor'), may hold values from -6 to 6
- token_counts: int32 [4], replicated, may hold values from 4096 to 16383
- due_index: int32 [1], replicated, may hold values from 0 to 39
Outputs:
- keys: bfloat16 [1024, 1024], P(('replica', 'fsdp'), 'tensor')
- key_weight_grad: bfloat16 [4, 8192, 1024], P('replica', 'fsdp', 'tensor')
- hidden_grad: bfloat16 [1024, 8192], P(('replica', 'fsdp'), 'tensor')
- fresh_params: bfloat16 [64, 1024], P('fsdp', 'tensor')
- fresh_moment: float32 [64, 1024], P(('fsdp', 'replica'), 'tensor')
All inputs are finite; a program needn't handle non-finite values.
Results may differ from a plain program's by a relative error of at most 0.009.
Values may be sent and summed in bfloat16 or wider, within the bound.
No kernel may reach another device: no remote copies, remote signals or barrier semaphores. Data moves between devices by JAX's collectives and lax.ppermute only.
A program may use at most 64 MiB of HBM per device.

v0:
```python
import jax
import jax.numpy as jnp
from jax import lax
from jax.sharding import PartitionSpec as P

outer_rate = 0.7
momentum_rate = 0.9


def on_device(
    hidden, key_weight, key_grad, pseudo_grads, outer_params, outer_moment, token_counts, due_index
):
    weight = key_weight[0]
    tok_rows = hidden.shape[0]
    shard_rows = weight.shape[0]
    head_cols = weight.shape[1]
    block_rows = lax.all_gather(weight, "fsdp", axis=0, tiled=True)
    key_sums = jnp.dot(hidden, block_rows, preferred_element_type=jnp.float32)
    product = lax.dot_general(
        key_grad, block_rows, (((1,), (1,)), ((), ())), preferred_element_type=jnp.float32
    )
    input_part = product.astype(jnp.bfloat16)
    key_sums, input_part = (key_sums, input_part)
    moved = lax.all_to_all(hidden, "fsdp", split_axis=1, concat_axis=0, tiled=True)
    cot_all = lax.all_gather(key_grad, "fsdp", axis=0, tiled=True)
    groups = lax.axis_size("fsdp")
    partial_value = jnp.einsum(
        "gtd,gth->gdh",
        moved.reshape(groups, tok_rows, shard_rows),
        cot_all.reshape(groups, tok_rows, head_cols),
        preferred_element_type=jnp.float32,
    )
    rounded = lax.optimization_barrier(partial_value.astype(jnp.bfloat16))
    weight_sum = jnp.sum(rounded.astype(jnp.float32), axis=0)
    input_sum = lax.psum_scatter(input_part, "tensor", scatter_dimension=1, tiled=True).astype(
        jnp.float32
    )
    keys = key_sums.astype(jnp.bfloat16)
    weight_grad = weight_sum.astype(jnp.bfloat16)[None]
    hidden_grad = input_sum.astype(jnp.bfloat16)
    counts = token_counts.astype(jnp.float32)
    replica_slot = lax.axis_index("replica")
    own_count = jnp.sum(jnp.where(jnp.arange(counts.shape[0]) == replica_slot, counts, 0.0))
    weight_share = own_count / jnp.sum(counts)
    average = lax.psum_scatter(
        pseudo_grads[0] * weight_share, "replica", scatter_dimension=0, tiled=True
    )
    due_slot = due_index[0]
    params_now = lax.dynamic_index_in_dim(outer_params, due_slot, 0, keepdims=False)
    moment_now = lax.dynamic_index_in_dim(outer_moment, due_slot, 0, keepdims=False)
    moment_new = momentum_rate * moment_now + average
    updated = params_now - outer_rate * (average + momentum_rate * moment_new)
    gathered = lax.all_gather(updated.astype(jnp.bfloat16), "replica", axis=0, tiled=True)
    return (keys, weight_grad, hidden_grad, gathered, moment_new)


def solution(mesh):
    return jax.shard_map(
        on_device,
        mesh=mesh,
        in_specs=(
            P(("replica", "fsdp"), None),
            P("replica", "fsdp", "tensor"),
            P(("replica", "fsdp"), "tensor"),
            P("replica", "fsdp", "tensor"),
            P(None, ("fsdp", "replica"), "tensor"),
            P(None, ("fsdp", "replica"), "tensor"),
            P(),
            P(),
        ),
        out_specs=(
            P(("replica", "fsdp"), "tensor"),
            P("replica", "fsdp", "tensor"),
            P(("replica", "fsdp"), "tensor"),
            P("fsdp", "tensor"),
            P(("fsdp", "replica"), "tensor"),
        ),
        check_vma=False,
    )
```

profile of v0, /device:TPU:0, one launch (start us, length us, event | category | flops | bytes accessed | tf_op | source)
XLA Modules:
  0.0 138.1 jit_solution(2214300956337062382)
XLA Ops:
  8.0 0.0 copy-start.3
  8.0 0.0 copy-start.2
  8.0 0.0 copy-start.1
  8.0 0.0 all-gather.3.cloned.1.call-start
  8.1 0.7 all-gather.3.cloned.1.call-update
  8.8 0.0 reduce-scatter.5.cloned.1.call-start
  8.8 0.0 copy-done.3
  8.8 0.6 convert_reduce_fusion
  10.8 0.0 copy-done.2
  10.8 0.6 multiply_bitcast_fusion
  11.4 0.0 reduce-scatter.5.cloned.1.call-update
  11.4 0.0 reduce-scatter.3.cloned.1.call-start
  11.5 58.4 %all-gather.3.cloned.1.call-done = bf16[1,8192,256]{2,1,0:T(8,128)(2,1)} async-done(((bf16[1,4096,256]{2,1,0:T(8,128)(2,1)}), bf16[1,8192,256]{2,1,0:T(8,128)(2,1)}) %all-gather.3.cloned.1.call-update) | async-done | bytes 4194320 | tf_op jit(solution)/shard_map/all_gather | solution.py:17
  69.9 0.0 copy-done.1
  69.9 5.0 %convolution_convert_fusion = bf16[128,8192]{1,0:T(8,128)(2,1)} fusion(bf16[128,256]{1,0:T(8,128)(2,1)S(1)} %copy-done.1, bf16[1,8192,256]{2,1,0:T(8,128)(2,1)} %all-gather.3.cloned.1.call-done), kind=kOutput, calls=%fused_computation | convolution fusion | flops 537919488 | bytes 6356992 | tf_op jit(solution)/shard_map/dot_general | solution.py:19
  74.9 0.0 copy-start
  74.9 0.0 reduce-scatter.3.cloned.1.call-update
  74.9 1.6 %copy-done = bf16[128,8192]{1,0:T(8,128)(2,1)S(1)} copy-done((bf16[128,8192]{1,0:T(8,128)(2,1)S(1)}, bf16[128,8192]{1,0:T(8,128)(2,1)}, u32[]{:S(2)}) %copy-start) | copy-done | bytes 2097176
  76.5 2.4 %copy.13 = bf16[128,8192]{0,1:T(8,128)(2,1)} copy(bf16[128,8192]{1,0:T(8,128)(2,1)S(1)} %copy-done) | data formatting | bytes 4194304 | tf_op args[0]
  78.9 4.9 %all-to-all-start = ((bf16[128,2,4096]{0,2,1:T(8,128)(2,1)}), bf16[128,2,4096]{0,2,1:T(8,128)(2,1)}, u32[]{:S(2)}, u32[]{:S(2)}) async-start(bf16[128,2,4096]{0,2,1:T(8,128)(2,1)} %bitcast.29), calls=%async_computation | async-start | bytes 4194304 | tf_op jit(solution)/shard_map/all_to_all | solution.py:24
  84.4 25.8 %all_gather.10 = bf16[256,256]{1,0:T(8,128)(2,1)S(1)} all-gather(bf16[128,256]{1,0:T(8,128)(2,1)S(1)} %copy-done.1), channel_id=1, replica_groups=mesh['replica'=4,'fsdp'=2,'tensor'=4] {'fsdp'}, dimensions={0}, use_global_device_ids=true | all-gather | bytes 196608 | tf_op jit(solution)/shard_map/all_gather | solution.py:25
  110.3 0.0 reduce-scatter.5.cloned.1.call-done
  110.3 1.3 fusion.7
  111.6 5.2 %all_gather.11 = bf16[32,256]{1,0:T(8,128)(2,1)S(1)} all-gather(bf16[8,256]{1,0:T(8,128)(2,1)S(1)} %get-tuple-element.7), channel_id=1, replica_groups=mesh['replica'=4,'fsdp'=2,'tensor'=4] {'replica'}, dimensions={0}, use_global_device_ids=true | all-gather | bytes 20480 | tf_op jit(solution)/shard_map/all_gather | solution.py:53
  116.8 0.0 all-to-all-done
  116.8 4.8 %convolution_convert_fusion.1 = bf16[2,4096,256]{2,1,0:T(8,128)(2,1)} fusion(bf16[2,128,256]{2,1,0:T(8,128)(2,1)S(1)} %bitcast.31, bf16[128,2,4096]{0,2,1:T(8,128)(2,1)} %all-to-all-done), kind=kOutput, calls=%fused_computation.1 | convolution fusion | flops 538968064 | bytes 6422528 | tf_op jit(solution)/shard_map/gtd,gth->gdh/dot_general | solution.py:27
  121.6 4.9 %reduce_sum.30 = bf16[4096,256]{1,0:T(8,128)(2,1)} reduce(bf16[2,4096,256]{2,1,0:T(8,128)(2,1)} %convolution_convert_fusion.1, bf16[]{:T(256)} %constant.14.clone.1), dimensions={0}, to_apply=%region_0.0 | reduce | flops 1048576 | bytes 6291458 | tf_op jit(solution)/shard_map/reduce_sum | solution.py:34
  126.5 3.5 %fusion.4 = bf16[128,256]{1,0:T(8,128)(2,1)} fusion(bf16[128,8192]{1,0:T(8,128)(2,1)S(1)} %copy-done, bf16[1,8192,256]{2,1,0:T(8,128)(2,1)} %all-gather.3.cloned.1.call-done), kind=kOutput, calls=%fused_computation.6 | convolution fusion | flops 536903680 | bytes 6356992 | tf_op jit(solution)/shard_map/dot_general | solution.py:18
  130.0 0.0 reduce-scatter.3.cloned.1.call-done
  130.0 0.6 copy.16
Async XLA Ops:
  8.0 0.8 copy-start.3
  8.0 2.8 %copy-start.2 = (f32[1,32,256]{2,1,0:T(8,128)S(1)}, f32[1,32,256]{2,1,0:T(8,128)}, u32[]{:S(2)}) copy-start(f32[1,32,256]{2,1,0:T(8,128)} %param.11) | copy-start | bytes 98308
  8.0 61.8 %copy-start.1 = (bf16[128,256]{1,0:T(8,128)(2,1)S(1)}, bf16[128,256]{1,0:T(8,128)(2,1)}, u32[]{:S(2)}) copy-start(bf16[128,256]{1,0:T(8,128)(2,1)} %param.10) | copy-start | bytes 196612
  8.0 61.8 %all-gather.3.cloned.1.call-start = ((), (), s32[]{:S(2)}) async-start(), calls=%async_computation.5 | async-start | bytes 6291456 | tf_op jit(solution)/shard_map/all_gather | solution.py:17
  8.8 101.5 %reduce-scatter.5.cloned.1.call-start = ((), (), s32[]{:S(2)}) async-start(), calls=%async_computation.4 | async-start | bytes 40960 | tf_op jit(solution)/shard_map/reduce_scatter | solution.py:45
  11.4 118.6 %reduce-scatter.3.cloned.1.call-start = ((), (), s32[]{:S(2)}) async-start(), calls=%async_computation.3 | async-start | bytes 2621440 | tf_op jit(solution)/shard_map/reduce_scatter | solution.py:35
  74.9 1.6 %copy-start = (bf16[128,8192]{1,0:T(8,128)(2,1)S(1)}, bf16[128,8192]{1,0:T(8,128)(2,1)}, u32[]{:S(2)}) copy-start(bf16[128,8192]{1,0:T(8,128)(2,1)} %param.8) | copy-start | bytes 6291460
  78.9 37.9 %all-to-all-start = ((bf16[128,2,4096]{0,2,1:T(8,128)(2,1)}), bf16[128,2,4096]{0,2,1:T(8,128)(2,1)}, u32[]{:S(2)}, u32[]{:S(2)}) async-start(bf16[128,2,4096]{0,2,1:T(8,128)(2,1)} %bitcast.29), calls=%async_computation | async-start | bytes 4194304 | tf_op jit(solution)/shard_map/all_to_all | solution.py:24
Sparse Core Ops, SparseCore 0:
  10.4 59.4 all-gather.2
Sparse Core Ops, SparseCore 1:
  12.2 22.2 reduce-scatter.4
  75.0 43.6 reduce-scatter.2
where the time goes:
time: 139 us; the launch traced here: 138 us
  waiting for transfers between devices  59.1 us (43%)
  blocking collectives  31 us (22%)
  between operations  17.5 us (13%)
  matrix products  13.4 us (10%)
  other arithmetic  7.45 us (5%)
  starting transfers between devices  4.99 us (4%)
  local copies, waits for them, and re-layouts  4.6 us (3%)
    all_gather x1, waiting for transfers between devices, on_device(): block_rows = lax.all_gather(weight, 'fsdp', axis=0, tiled=True)  58.4 us
    all_gather x1, blocking collectives, on_device(): cot_all = lax.all_gather(key_grad, 'fsdp', axis=0, tiled=True)  25.8 us
    all_gather x1, blocking collectives, on_device(): lax.all_gather(updated.astype(jnp.bfloat16), 'replica', axis=0, tiled=True)  5.19 us
    dot_general x1, matrix products, on_device(): lax.dot_general(key_grad, block_rows, (((1,), (1,)), ((), ())), preferred...  5.05 us
    reduce_sum x1, other arithmetic, on_device(): weight_sum = jnp.sum(rounded.astype(jnp.float32), axis=0)  4.89 us
    all_to_all x1, starting transfers between devices, on_device(): lax.all_to_all(hidden, 'fsdp', split_axis=1, concat_axis=0, tiled=True)  4.87 us
    dot_general x1, matrix products, on_device(): jnp.einsum('gtd,gth->gdh', moved.reshape(groups, tok_rows, shard_rows), c...  4.8 us
    unnamed x10, local copies, waits for them, and re-layouts  4.6 us
  transfers between devices with their start and end apart: 4, of which 1 were waited for; matrix products, arithmetic and copies ran while one was open for 17% of the time, Pallas kernels for 0%

commit v1 on v0

v1 whole, which is shorter than its diff:
```python
import functools
import math

import jax
import jax.numpy as jnp
from jax import lax
from jax.experimental import pallas as pl
from jax.experimental.pallas import tpu as pltpu
from jax.sharding import PartitionSpec as P

outer_rate = 0.7
momentum_rate = 0.9
PARTS = (6, 6, 4)
LOAD_LIMIT = 50
GRADS = ((0, 1), (2,))
FINALS = ((0, 1), (2,))
PIECES = (3, 3, 2)


def matmul_t(a, b):
    return lax.dot_general(a, b, (((1,), (1,)), ((), ())), preferred_element_type=jnp.float32)


def matmul_first(a, b):
    return lax.dot_general(a, b, (((0,), (0,)), ((), ())), preferred_element_type=jnp.float32)


def flip(value, axis, bit):
    size = lax.axis_size(axis)
    return lax.ppermute(value, axis, [(i, i ^ bit) for i in range(size)])


def share_of(token_counts):
    counts = token_counts.astype(jnp.float32)
    replica_slot = lax.axis_index("replica")
    own_count = jnp.sum(jnp.where(jnp.arange(counts.shape[0]) == replica_slot, counts, 0.0))
    return own_count / jnp.sum(counts)


def stepped(average, params_now, moment_now):
    moment_new = momentum_rate * moment_now + average
    updated = params_now - outer_rate * (average + momentum_rate * moment_new)
    return updated.astype(jnp.bfloat16), moment_new


def due_rows(outer_params, outer_moment, due_index):
    due_slot = due_index[0]
    params_now = lax.dynamic_index_in_dim(outer_params, due_slot, 0, keepdims=False)
    moment_now = lax.dynamic_index_in_dim(outer_moment, due_slot, 0, keepdims=False)
    return params_now, moment_now


VMEM = pl.BlockSpec(memory_space=pltpu.VMEM)
HBM = pl.BlockSpec(memory_space=pltpu.HBM)
SMEM = pl.BlockSpec(memory_space=pltpu.SMEM)


def call(kernel, out_shape, in_specs, out_specs, scratch=(), aliases=None, flops=0, limit=10):
    def run(*arrays):
        return pl.pallas_call(
            kernel,
            out_shape=out_shape,
            in_specs=in_specs,
            out_specs=out_specs,
            scratch_shapes=scratch,
            input_output_aliases=aliases or {},
            compiler_params=pltpu.CompilerParams(vmem_limit_bytes=limit * 2**20),
            cost_estimate=pl.CostEstimate(flops=flops, bytes_accessed=2**20, transcendentals=0),
        )(*arrays)

    return run


def load_kernel(hidden, weight, sent, weight_out, sems):
    start = pl.multiple_of((1 - lax.axis_index("fsdp")) * weight.shape[0], 128)
    copies = [
        pltpu.make_async_copy(hidden.at[:, pl.ds(start, sent.shape[1])], sent, sems.at[0]),
        pltpu.make_async_copy(weight, weight_out, sems.at[1]),
    ]
    for copy in copies:
        copy.start()
    for copy in copies:
        copy.wait()


def late_load_kernel(rows, base, hidden, sent, sem):
    start = pl.multiple_of((1 - lax.axis_index("fsdp")) * rows + base, 128)
    copy = pltpu.make_async_copy(hidden.at[:, pl.ds(start, sent.shape[1])], sent, sem)
    copy.start()
    copy.wait()


def sent_kernel(weight, own, other, *outs):
    block = sum(out.shape[1] for out in outs) // 2
    offset = (1 - lax.axis_index("tensor") % 2) * block
    for i, out in enumerate(outs):
        if i == len(outs) // 2:
            offset = offset - block
        rows = weight[pl.ds(pl.multiple_of(offset, 128), out.shape[1]), :]
        out[...] = matmul_t((other if i < len(outs) // 2 else own)[...], rows).astype(out.dtype)
        offset = offset + out.shape[1]


def kept_kernel(weight, own, other, *outs):
    tokens = own.shape[0]
    offset = (lax.axis_index("tensor") % 2) * sum(out.shape[1] for out in outs)
    for out in outs:
        rows = weight[pl.ds(pl.multiple_of(offset, 128), out.shape[1]), :]
        out[:tokens] = matmul_t(own[...], rows)
        out[tokens:] = matmul_t(other[...], rows)
        offset = offset + out.shape[1]


def others_kernel(kept, got, out):
    out[...] = (kept[out.shape[0] :] + got[...].astype(jnp.float32)).astype(out.dtype)


def at_home(shape):
    home = (lax.axis_index("fsdp") == lax.axis_index("tensor") // 2).astype(jnp.int32)
    return jnp.full(shape, home, jnp.int32) == 1


def select_kernel(kept, got, crossed, away, stay):
    mine = (kept[: away.shape[0]] + got[...].astype(jnp.float32)).astype(away.dtype)
    home = at_home(away.shape)
    away[...] = jnp.where(home, crossed[...], mine)
    stay[...] = jnp.where(home, mine, crossed[...])


def final_parts(base, parts, out, made, sems):
    copies, offset = [], 0
    for i in range(len(parts) // 2):
        stay, last = parts[2 * i : 2 * i + 2]
        columns = pl.ds(offset, stay.shape[1])
        total = stay[...].astype(jnp.float32) + last[...].astype(jnp.float32)
        made[:, columns] = total.astype(made.dtype)
        where = pl.ds(base + offset, stay.shape[1])
        copies.append(pltpu.make_async_copy(made.at[:, columns], out.at[:, where], sems.at[i]))
        copies[i].start()
        offset += stay.shape[1]
    return copies


def final_kernel(base, count, *refs):
    for copy in final_parts(base, refs[: 2 * count], *refs[-3:]):
        copy.wait()


def last_kernel(base, count, *refs):
    parts, (own_part, back, packed, got) = refs[: 2 * count], refs[2 * count : 2 * count + 4]
    out, keys, params_out, moment_out, made, sems = refs[-6:]
    copies = final_parts(base, parts, out, made, sems)
    keys[...] = (own_part[...] + back[...].astype(jnp.float32)).astype(keys.dtype)
    outer_last(params_out.shape[0], moment_out.shape[0], packed, got, params_out, moment_out)
    for copy in copies:
        copy.wait()


def weights_kernel(base, width, count, hidden, own_cot, other_cot, *rest):
    moved, (out, left, made, sems) = rest[:count], rest[-4:]
    start = pl.multiple_of(lax.axis_index("fsdp") * out.shape[0] + base, 128)
    blocks = [(piece, at) for piece in moved for at in range(0, piece.shape[1], width)]
    reads, writes = [], []
    for b in range(len(blocks)):
        columns = pl.ds(start + b * width, width)
        reads.append(pltpu.make_async_copy(hidden.at[:, columns], left.at[b], sems.at[0, b]))
        reads[b].start()
    for b, (piece, at) in enumerate(blocks):
        reads[b].wait()
        right = piece[:, at : at + width]
        total = matmul_first(left[b], own_cot[...]) + matmul_first(right, other_cot[...])
        made[b] = total.astype(made.dtype)
        writes.append(
            pltpu.make_async_copy(made.at[b], out.at[pl.ds(base + b * width, width)], sems.at[1, b])
        )
        writes[b].start()
    for copy in writes:
        copy.wait()


def weight_rows(hidden, moved, own_cot, other_cot, rows, base, before):
    tokens, head_cols = own_cot.shape
    columns = sum(piece.shape[1] for piece in moved)
    width = math.gcd(512, *(piece.shape[1] for piece in moved))
    blocks = columns // width
    kept = () if before is None else (before,)
    run = call(
        functools.partial(weights_kernel, base, width, len(moved)),
        jax.ShapeDtypeStruct((rows, head_cols), jnp.bfloat16),
        [HBM] + [VMEM] * (2 + len(moved)) + [HBM] * len(kept),
        HBM,
        [
            pltpu.VMEM((blocks, tokens, width), hidden.dtype),
            pltpu.VMEM((blocks, width, head_cols), jnp.bfloat16),
            pltpu.SemaphoreType.DMA((2, blocks)),
        ],
        {3 + len(moved): 0} if kept else {},
        4 * tokens * head_cols * columns,
    )
    return run(hidden, own_cot, other_cot, *moved, *kept)


def keys_own_kernel(hidden, moved, weight, own_part, moved_part, left, sem):
    start = pl.multiple_of(lax.axis_index("fsdp") * weight.shape[0], 128)
    copy = pltpu.make_async_copy(hidden.at[:, pl.ds(start, left.shape[1])], left, sem)
    copy.start()
    half = moved.shape[1]
    moved_part[...] = jnp.dot(moved[...], weight[:half], preferred_element_type=jnp.float32)
    copy.wait()
    own_part[...] = jnp.dot(left[...], weight[...], preferred_element_type=jnp.float32)


def keys_sent_kernel(part, weight, *rest):
    moved, out = rest[:-1], rest[-1]
    total = part[...]
    base = weight.shape[0] - sum(piece.shape[1] for piece in moved)
    for piece in moved:
        rows = weight[base : base + piece.shape[1]]
        total = total + jnp.dot(piece[...], rows, preferred_element_type=jnp.float32)
        base += piece.shape[1]
    out[...] = total.astype(out.dtype)


def outer_first_kernel(due_index, counts, grads, params, moment, packed, sems):
    rows, own = grads.shape[0], params.shape[1]
    due, slot = due_index[0], lax.axis_index("replica")
    reads = [
        pltpu.make_async_copy(source.at[due], packed.at[pl.ds(rows + i * own, own)], sems.at[i])
        for i, source in enumerate((params, moment))
    ]
    for copy in reads:
        copy.start()
    total = jnp.float32(0)
    for i in range(counts.shape[0]):
        total = total + counts[i].astype(jnp.float32)
    shape = (1, grads.shape[1])
    share = jnp.full(shape, counts[slot].astype(jnp.float32)) / jnp.full(shape, total)
    packed[:rows] = grads[...] * share
    for copy in reads:
        copy.wait()


def lower_half(bit, shape):
    mine = (lax.axis_index("replica") // bit) % 2
    return jnp.full(shape, mine, jnp.int32) == 0


def outer_join_kernel(rows, packed, got, out):
    held = packed.shape[0] - rows
    out[:rows] = packed[:rows] + got[:rows]
    here = lower_half(1, (held, packed.shape[1]))
    out[rows : rows + held] = jnp.where(here, packed[rows:], got[rows:])
    out[rows + held :] = jnp.where(here, got[rows:], packed[rows:])


def outer_last(rows, own, packed, got, params_out, moment_out):
    average = packed[:rows] + got[:rows]
    owners = rows // own
    here = lower_half(2, (2 * own, packed.shape[1]))
    for i in range(owners):
        low = i < owners // 2
        base = rows + (i % (owners // 2)) * 2 * own
        ours, theirs = packed[base : base + 2 * own], got[base : base + 2 * own]
        held = jnp.where(here, ours, theirs) if low else jnp.where(here, theirs, ours)
        part = average[i * own : (i + 1) * own]
        updated, moment_new = stepped(part, held[:own], held[own:])
        params_out[i * own : (i + 1) * own] = updated

        @pl.when(lax.axis_index("replica") == i)
        def _():
            moment_out[...] = moment_new


def outer_step(pseudo_grads, outer_params, outer_moment, token_counts, due_index):
    grads = pseudo_grads[0]
    rows, columns = grads.shape
    own = outer_params.shape[1]

    def packed_shape(owners):
        return jax.ShapeDtypeStruct((rows + 2 * own * owners, columns), jnp.float32)

    specs = [SMEM, SMEM, VMEM, HBM, HBM]
    sems = [pltpu.SemaphoreType.DMA((2,))]
    packed = call(outer_first_kernel, packed_shape(1), specs, VMEM, sems)(
        due_index, token_counts, grads, outer_params, outer_moment
    )
    got = flip(packed, "replica", 1)
    kernel = functools.partial(outer_join_kernel, rows)
    packed = call(kernel, packed_shape(2), [VMEM, VMEM], VMEM)(packed, got)
    got = flip(packed, "replica", 2)
    outs = (
        jax.ShapeDtypeStruct((rows, columns), jnp.bfloat16),
        jax.ShapeDtypeStruct((own, columns), jnp.float32),
    )
    return packed, got, outs


def on_device(
    hidden, key_weight, key_grad, pseudo_grads, outer_params, outer_moment, token_counts, due_index
):
    shard_rows, head_cols = key_weight.shape[1:]
    tok_rows = key_grad.shape[0]
    widths = [shard_rows * piece // sum(PIECES) for piece in PIECES]
    bases = [sum(widths[:i]) for i in range(len(widths))]
    other_cot = flip(key_grad, "fsdp", 1)
    narrow = jax.ShapeDtypeStruct((tok_rows, widths[0]), hidden.dtype)
    outs = (narrow, jax.ShapeDtypeStruct((shard_rows, head_cols), key_weight.dtype))
    sems = [pltpu.SemaphoreType.DMA((2,))]
    sent, weight = call(load_kernel, outs, [HBM] * 2, (VMEM,) * 2, sems, limit=LOAD_LIMIT)(
        hidden, key_weight[0]
    )
    moved = [flip(sent, "fsdp", 1)]
    for i in range(1, len(widths)):
        narrow = jax.ShapeDtypeStruct((tok_rows, widths[i]), hidden.dtype)
        kernel = functools.partial(late_load_kernel, shard_rows, bases[i])
        sent = call(kernel, narrow, [HBM], VMEM, [pltpu.SemaphoreType.DMA])(hidden)
        moved.append(flip(sent, "fsdp", 1))

    block = shard_rows // 2
    chunks = [block * part // sum(PARTS) for part in PARTS]
    count, flops = len(chunks), 4 * tok_rows * head_cols * block
    part = [jax.ShapeDtypeStruct((tok_rows, chunk), jnp.bfloat16) for chunk in chunks]
    both = [jax.ShapeDtypeStruct((2 * tok_rows, chunk), jnp.float32) for chunk in chunks]
    inputs = (weight, key_grad, other_cot)
    gone = call(sent_kernel, part * 2, [VMEM] * 3, [VMEM] * (2 * count), flops=flops)(*inputs)
    kept = call(kept_kernel, both, [VMEM] * 3, [VMEM] * count, flops=flops)(*inputs)
    got = [flip(gone[c], "tensor", 1) for c in range(count)]
    got_own = [flip(gone[count + c], "tensor", 1) for c in range(count)]
    ends = []
    for c in range(count):
        others = call(others_kernel, part[c], [VMEM] * 2, VMEM)(kept[c], got[c])
        crossed = flip(others, "fsdp", 1)
        run = call(select_kernel, (part[c],) * 2, [VMEM] * 3, (VMEM,) * 2)
        away, stay = run(kept[c], got_own[c], crossed)
        ends.append((stay, flip(away, "tensor", 2)))
    sums = jax.ShapeDtypeStruct((tok_rows, head_cols), jnp.float32)
    own_part, moved_part = call(
        keys_own_kernel,
        (sums, sums),
        [HBM, VMEM, VMEM],
        (VMEM, VMEM),
        [pltpu.VMEM((tok_rows, shard_rows), hidden.dtype), pltpu.SemaphoreType.DMA],
    )(hidden, moved[0], weight)
    part = jax.ShapeDtypeStruct((tok_rows, head_cols), jnp.bfloat16)
    sums_sent = call(keys_sent_kernel, part, [VMEM] * (1 + len(moved)), VMEM)(
        moved_part, weight, *moved[1:]
    )
    back = flip(sums_sent, "fsdp", 1)

    weight_grad = None
    for group in GRADS:
        pieces = [moved[p] for p in group]
        weight_grad = weight_rows(
            hidden, pieces, key_grad, other_cot, shard_rows, bases[group[0]], weight_grad
        )

    outer, outer_got, outer_outs = outer_step(
        pseudo_grads, outer_params, outer_moment, token_counts, due_index
    )

    hidden_grad, base = None, 0
    for i, group in enumerate(FINALS):
        ending = i == len(FINALS) - 1
        before = () if hidden_grad is None else (hidden_grad,)
        parts = [array for c in group for array in ends[c]]
        width = sum(chunks[c] for c in group)
        extra = (own_part, back, outer, outer_got) if ending else ()
        outs = (jax.ShapeDtypeStruct((tok_rows, block), jnp.bfloat16),)
        kernel = functools.partial(final_kernel, base, len(group))
        if ending:
            outs += (part, *outer_outs)
            kernel = functools.partial(last_kernel, base, len(group))
        run = call(
            kernel,
            outs,
            [VMEM] * (len(parts) + len(extra)) + [HBM] * len(before),
            (HBM,) + (VMEM,) * (len(outs) - 1),
            [pltpu.VMEM((tok_rows, width), jnp.bfloat16), pltpu.SemaphoreType.DMA((len(group),))],
            {len(parts) + len(extra): 0} if before else {},
        )
        hidden_grad, *others = run(*parts, *extra, *before)
        base += width
    keys, fresh_params, fresh_moment = others
    return (keys, weight_grad[None], hidden_grad, fresh_params, fresh_moment)


def on_device_any(
    hidden, key_weight, key_grad, pseudo_grads, outer_params, outer_moment, token_counts, due_index
):
    weight = key_weight[0]
    block_rows = lax.all_gather(weight, "fsdp", axis=0, tiled=True)
    keys = jnp.dot(hidden, block_rows, preferred_element_type=jnp.float32).astype(jnp.bfloat16)
    input_part = matmul_t(key_grad, block_rows).astype(jnp.bfloat16)
    moved = lax.all_to_all(hidden, "fsdp", split_axis=1, concat_axis=0, tiled=True)
    cot_all = lax.all_gather(key_grad, "fsdp", axis=0, tiled=True)
    weight_grad = matmul_first(moved, cot_all).astype(jnp.bfloat16)[None]
    hidden_grad = lax.psum_scatter(input_part, "tensor", scatter_dimension=1, tiled=True)
    average = lax.psum_scatter(
        pseudo_grads[0] * share_of(token_counts), "replica", scatter_dimension=0, tiled=True
    )
    updated, moment_new = stepped(average, *due_rows(outer_params, outer_moment, due_index))
    gathered = lax.all_gather(updated, "replica", axis=0, tiled=True)
    return (keys, weight_grad, hidden_grad, gathered, moment_new)


def solution(mesh):
    sizes = mesh.shape
    fits = sizes["fsdp"] == 2 and sizes["tensor"] == 4 and sizes["replica"] == 4

    def step(*arrays):
        return (on_device if fits else on_device_any)(*arrays)

    return jax.shard_map(
        step,
        mesh=mesh,
        in_specs=(
            P(("replica", "fsdp"), None),
            P("replica", "fsdp", "tensor"),
            P(("replica", "fsdp"), "tensor"),
            P("replica", "fsdp", "tensor"),
            P(None, ("fsdp", "replica"), "tensor"),
            P(None, ("fsdp", "replica"), "tensor"),
            P(),
            P(),
        ),
        out_specs=(
            P(("replica", "fsdp"), "tensor"),
            P("replica", "fsdp", "tensor"),
            P(("replica", "fsdp"), "tensor"),
            P("fsdp", "tensor"),
            P(("fsdp", "replica"), "tensor"),
        ),
        check_vma=False,
    )
```

time: 139 us -> 64.5 us (0.46)
  waiting for transfers between devices: 59.1 us -> 20.4 us
  blocking collectives: 31 us -> 0 us
  starting transfers between devices: 4.99 us -> 29.2 us
  between operations: 17.5 us -> 1.56 us
  matrix products: 13.4 us -> 0 us
  Pallas kernels: 0 us -> 13.1 us
  other arithmetic: 7.45 us -> 0 us
  local copies, waits for them, and re-layouts: 4.6 us -> 0.04 us
    all_gather x1 -> x0, waiting for transfers between devices: 58.4 us -> none  [on_device(): block_rows = lax.all_gather(weight, 'fsdp', axis=0, tiled=True)]
    all_gather x2 -> x0, blocking collectives: 31 us -> none  [the longest x1 25.8 us: on_device(): cot_all = lax.all_gather(key_grad, 'fsdp', axis=0, tiled=True)]
    ppermute x0 -> x19, starting transfers between devices: none -> 29.2 us  [flip(): return lax.ppermute(value, axis, [(i, i ^ bit) for i in range(size)])]
    ppermute x0 -> x19, waiting for transfers between devices: none -> 20.4 us  [flip(): return lax.ppermute(value, axis, [(i, i ^ bit) for i in range(size)])]
    dot_general x3 -> x0, matrix products: 13.4 us -> none  [the longest x1 5.05 us: on_device(): lax.dot_general(key_grad, block_rows, (((1,), (1,)), ((), ())), preferred...]
    pallas_call x0 -> x19, Pallas kernels: none -> 13.1 us  [run(): pl.pallas_call(kernel, out_shape=out_shape, in_specs=in_specs, out_specs=...]
    reduce_sum x2 -> x0, other arithmetic: 5.5 us -> none  [the longest x1 4.89 us: on_device(): weight_sum = jnp.sum(rounded.astype(jnp.float32), axis=0)]
    all_to_all x1 -> x0, starting transfers between devices: 4.87 us -> none  [on_device(): lax.all_to_all(hidden, 'fsdp', split_axis=1, concat_axis=0, tiled=True)]
  transfers between devices with their start and end apart: 4 -> 19, of which waited for: 1 -> 8; matrix products, arithmetic and copies ran while one was open for 17% -> 0% of each run, Pallas kernels for 0% -> 17%
where the time goes in v1:
time: 64.5 us; the launch traced here: 64.3 us
  starting transfers between devices  29.2 us (45%)
  waiting for transfers between devices  20.4 us (32%)
  Pallas kernels  13.1 us (20%)
  between operations  1.56 us (2%)
    ppermute x19, starting transfers between devices, flip(): return lax.ppermute(value, axis, [(i, i ^ bit) for i in range(size)])  29.2 us
    ppermute x19, waiting for transfers between devices, flip(): return lax.ppermute(value, axis, [(i, i ^ bit) for i in range(size)])  20.4 us
    pallas_call x19, Pallas kernels, run(): pl.pallas_call(kernel, out_shape=out_shape, in_specs=in_specs, out_specs=...  13.1 us
  transfers between devices with their start and end apart: 19, of which 8 were waited for; matrix products, arithmetic and copies ran while one was open for 0% of the time, Pallas kernels for 17%

profile of v1, /device:TPU:0, one launch (start us, length us, event | category | flops | bytes accessed | tf_op | source)
XLA Modules:
  0.0 64.3 jit_solution(4395592837880993295)
XLA Ops:
  0.6 3.0 %collective-permute-start = (bf16[128,256]{1,0:T(8,128)(2,1)}, bf16[128,256]{1,0:T(8,128)(2,1)S(1)}, u32[]{:S(2)}, u32[]{:S(2)}) collective-permute-start(bf16[128,256]{1,0:T(8,128)(2,1)} %own_cot.3), channel_id=1, source_target_pairs={{0,4},{4,0},{1,5},{5,1},{2,6},{6,2},{3,7},{7,3},{8,12},{12,8},{9,1... | collective-permute-start | bytes 196616 | tf_op jit(solution)/shard_map/ppermute | solution.py:30
  3.7 1.8 %shard_map.119 = (bf16[128,1536]{1,0:T(8,128)(2,1)S(1)}, bf16[4096,256]{1,0:T(8,128)(2,1)S(1)}) custom-call(bf16[128,8192]{1,0:T(8,128)(2,1)} %hidden.11, bf16[4096,256]{1,0:T(8,128)(2,1)} %bitcast.5), custom_call_target="tpu_custom_call" | custom-call | bytes 1048576 | tf_op jit(solution)/shard_map/pallas_call | solution.py:60
  5.4 0.0 copy-start.2
  5.5 0.0 copy-start.3
  5.5 0.0 copy-start.4
  5.5 0.0 copy-start.5
  5.5 0.6 collective-permute-done.other.other_cot
  6.1 0.8 %shard_map.121 = (bf16[128,768]{1,0:T(8,128)(2,1)S(1)}, bf16[128,768]{1,0:T(8,128)(2,1)S(1)}, bf16[128,512]{1,0:T(8,128)(2,1)S(1)}, bf16[128,768]{1,0:T(8,128)(2...) custom-call(bf16[4096,256]{1,0:T(8,128)(2,1)S(1)} %get-tuple-element.28.weight, ...), custom_call_target="tpu_custom_call" | custom-call | flops 268435456 | bytes 1048576 | tf_op jit(solution)/shard_map/pallas_call | solution.py:60
  6.9 2.2 %collective-permute-start.16 = (bf16[128,768]{1,0:T(8,128)(2,1)S(1)}, bf16[128,768]{1,0:T(8,128)(2,1)S(1)}, u32[]{:S(2)}, u32[]{:S(2)}) collective-permute-start(bf16[128,768]{1,0:T(8,128)(2,1)S(1)} %get-tuple-element.44), channel_id=1, source_target_pairs={{0,1},{1,0},{2,3},{3,2},{4,5},{5,4},{6,7},{7,6},{8,9},{9,8},{10,11... | collective-permute-start | bytes 589832 | tf_op jit(solution)/shard_map/ppermute | solution.py:30
  9.1 0.1 collective-permute-start.12
  9.2 1.9 %collective-permute-start.2 = (bf16[128,512]{1,0:T(8,128)(2,1)S(1)}, bf16[128,512]{1,0:T(8,128)(2,1)S(1)}, u32[]{:S(2)}, u32[]{:S(2)}) collective-permute-start(bf16[128,512]{1,0:T(8,128)(2,1)S(1)} %get-tuple-element.31), channel_id=1, source_target_pairs={{0,1},{1,0},{2,3},{3,2},{4,5},{5,4},{6,7},{7,6},{8,9},{9,8},{10,11... | collective-permute-start | bytes 393224 | tf_op jit(solution)/shard_map/ppermute | solution.py:30
  11.1 0.1 collective-permute-start.15
  11.9 0.6 shard_map.128.packed
  12.5 0.0 copy-start
  12.5 0.1 collective-permute-start.9
  12.6 0.8 %shard_map.120 = (f32[256,768]{1,0:T(8,128)S(1)}, f32[256,768]{1,0:T(8,128)S(1)}, f32[256,512]{1,0:T(8,128)S(1)}) custom-call(bf16[4096,256]{1,0:T(8,128)(2,1)S(1)} %get-tuple-element.28.weight, bf16[128,256]{1,0:T(8,128)(2,1)S(1)} %copy-done.1, bf16[128,256]{1,0:T(8,128)(2,1)S(1)} %collective-permute-done.other.other_cot), custom_call_target="tpu_custom_call" | custom-call | flops 268435456 | bytes 1048576 | tf_op jit(solution)/shard_map/pallas_call | solution.py:60
  13.4 1.4 %collective-permute-done.16.got = bf16[128,768]{1,0:T(8,128)(2,1)S(1)} collective-permute-done((bf16[128,768]{1,0:T(8,128)(2,1)S(1)}, bf16[128,768]{1,0:T(8,128)(2,1)S(1)}, u32[]{:S(2)}, u32[]{:S(2)}) %collective-permute-start.16) | collective-permute-done | bytes 196640 | tf_op jit(solution)/shard_map/ppermute | solution.py:30
  14.9 2.0 %collective-permute-start.11 = (bf16[128,768]{1,0:T(8,128)(2,1)S(1)}, bf16[128,768]{1,0:T(8,128)(2,1)S(1)}, u32[]{:S(2)}, u32[]{:S(2)}) collective-permute-start(bf16[128,768]{1,0:T(8,128)(2,1)S(1)} %get-tuple-element.38), channel_id=1, source_target_pairs={{0,1},{1,0},{2,3},{3,2},{4,5},{5,4},{6,7},{7,6},{8,9},{9,8},{10,11... | collective-permute-start | bytes 589832 | tf_op jit(solution)/shard_map/ppermute | solution.py:30
  16.9 2.2 %collective-permute-done.12.got = bf16[128,768]{1,0:T(8,128)(2,1)S(1)} collective-permute-done((bf16[128,768]{1,0:T(8,128)(2,1)S(1)}, bf16[128,768]{1,0:T(8,128)(2,1)S(1)}, u32[]{:S(2)}, u32[]{:S(2)}) %collective-permute-start.12) | collective-permute-done | bytes 196640 | tf_op jit(solution)/shard_map/ppermute | solution.py:30
  19.1 1.9 %collective-permute-start.17 = (bf16[128,768]{1,0:T(8,128)(2,1)S(1)}, bf16[128,768]{1,0:T(8,128)(2,1)S(1)}, u32[]{:S(2)}, u32[]{:S(2)}) collective-permute-start(bf16[128,768]{1,0:T(8,128)(2,1)S(1)} %shard_map.132), channel_id=1, source_target_pairs={{0,4},{4,0},{1,5},{5,1},{2,6},{6,2},{3,7},{7,3},{8,12},{12,8},{9,1... | collective-permute-start | bytes 589832 | tf_op jit(solution)/shard_map/ppermute | solution.py:30
  21.1 0.2 collective-permute-start.13
  21.2 0.7 %collective-permute-done.2.got = bf16[128,512]{1,0:T(8,128)(2,1)S(1)} collective-permute-done((bf16[128,512]{1,0:T(8,128)(2,1)S(1)}, bf16[128,512]{1,0:T(8,128)(2,1)S(1)}, u32[]{:S(2)}, u32[]{:S(2)}) %collective-permute-start.2) | collective-permute-done | bytes 131104 | tf_op jit(solution)/shard_map/ppermute | solution.py:30
  21.9 1.9 %collective-permute-start.5 = (bf16[128,1536]{1,0:T(8,128)(2,1)S(1)}, bf16[128,1536]{1,0:T(8,128)(2,1)S(1)}, u32[]{:S(2)}, u32[]{:S(2)}) collective-permute-start(bf16[128,1536]{1,0:T(8,128)(2,1)S(1)} %get-tuple-element.34), channel_id=1, source_target_pairs={{0,4},{4,0},{1,5},{5,1},{2,6},{6,2},{3,7},{7,3},{8,12},{12,8},{9,1... | collective-permute-start | bytes 1179656 | tf_op jit(solution)/shard_map/ppermute | solution.py:30
  23.9 2.2 %collective-permute-done.15.got = bf16[128,768]{1,0:T(8,128)(2,1)S(1)} collective-permute-done((bf16[128,768]{1,0:T(8,128)(2,1)S(1)}, bf16[128,768]{1,0:T(8,128)(2,1)S(1)}, u32[]{:S(2)}, u32[]{:S(2)}) %collective-permute-start.15) | collective-permute-done | bytes 196640 | tf_op jit(solution)/shard_map/ppermute | solution.py:30
  26.1 1.8 %collective-permute-start.6 = (bf16[128,1536]{1,0:T(8,128)(2,1)S(1)}, bf16[128,1536]{1,0:T(8,128)(2,1)S(1)}, u32[]{:S(2)}, u32[]{:S(2)}) collective-permute-start(bf16[128,1536]{1,0:T(8,128)(2,1)S(1)} %shard_map.125), channel_id=1, source_target_pairs={{0,4},{4,0},{1,5},{5,1},{2,6},{6,2},{3,7},{7,3},{8,12},{12,8},{9,1... | collective-permute-start | bytes 1179656 | tf_op jit(solution)/shard_map/ppermute | solution.py:30
  27.9 0.4 collective-permute-done.11.got
  28.3 1.7 %collective-permute-start.1 = (bf16[128,512]{1,0:T(8,128)(2,1)S(1)}, bf16[128,512]{1,0:T(8,128)(2,1)S(1)}, u32[]{:S(2)}, u32[]{:S(2)}) collective-permute-start(bf16[128,512]{1,0:T(8,128)(2,1)S(1)} %get-tuple-element.30), channel_id=1, source_target_pairs={{0,1},{1,0},{2,3},{3,2},{4,5},{5,4},{6,7},{7,6},{8,9},{9,8},{10,11... | collective-permute-start | bytes 393224 | tf_op jit(solution)/shard_map/ppermute | solution.py:30
  30.1 0.0 collective-permute-done.17.crossed
  30.1 1.6 %collective-permute-start.3 = (bf16[128,512]{1,0:T(8,128)(2,1)S(1)}, bf16[128,512]{1,0:T(8,128)(2,1)S(1)}, u32[]{:S(2)}, u32[]{:S(2)}) collective-permute-start(bf16[128,512]{1,0:T(8,128)(2,1)S(1)} %shard_map.122), channel_id=1, source_target_pairs={{0,4},{4,0},{1,5},{5,1},{2,6},{6,2},{3,7},{7,3},{8,12},{12,8},{9,1... | collective-permute-start | bytes 393224 | tf_op jit(solution)/shard_map/ppermute | solution.py:30
  31.7 0.0 collective-permute-done.13.crossed
  31.7 1.3 %collective-permute-start.7 = (bf16[128,1024]{1,0:T(8,128)(2,1)S(1)}, bf16[128,1024]{1,0:T(8,128)(2,1)S(1)}, u32[]{:S(2)}, u32[]{:S(2)}) collective-permute-start(bf16[128,1024]{1,0:T(8,128)(2,1)S(1)} %shard_map.126), channel_id=1, source_target_pairs={{0,4},{4,0},{1,5},{5,1},{2,6},{6,2},{3,7},{7,3},{8,12},{12,8},{9,1... | collective-permute-start | bytes 786440 | tf_op jit(solution)/shard_map/ppermute | solution.py:30
  33.0 0.1 shard_map.133
  33.1 0.1 shard_map.131
  33.2 0.1 collective-permute-done.1.got
  33.3 3.3 %collective-permute-start.18 = (bf16[128,768]{1,0:T(8,128)(2,1)S(1)}, bf16[128,768]{1,0:T(8,128)(2,1)S(1)}, u32[]{:S(2)}, u32[]{:S(2)}) collective-permute-start(bf16[128,768]{1,0:T(8,128)(2,1)S(1)} %get-tuple-element.46), channel_id=1, source_target_pairs={{0,2},{1,3},{2,0},{3,1},{4,6},{5,7},{6,4},{7,5},{8,10},{9,11},{10,... | collective-permute-start | bytes 589832 | tf_op jit(solution)/shard_map/ppermute | solution.py:30
  36.6 12.7 %collective-permute-done.3.crossed = bf16[128,512]{1,0:T(8,128)(2,1)S(1)} collective-permute-done((bf16[128,512]{1,0:T(8,128)(2,1)S(1)}, bf16[128,512]{1,0:T(8,128)(2,1)S(1)}, u32[]{:S(2)}, u32[]{:S(2)}) %collective-permute-start.3) | collective-permute-done | bytes 131104 | tf_op jit(solution)/shard_map/ppermute | solution.py:30
  49.3 2.6 %collective-permute-start.14 = (bf16[128,768]{1,0:T(8,128)(2,1)S(1)}, bf16[128,768]{1,0:T(8,128)(2,1)S(1)}, u32[]{:S(2)}, u32[]{:S(2)}) collective-permute-start(bf16[128,768]{1,0:T(8,128)(2,1)S(1)} %get-tuple-element.41), channel_id=1, source_target_pairs={{0,2},{1,3},{2,0},{3,1},{4,6},{5,7},{6,4},{7,5},{8,10},{9,11},{10,... | collective-permute-start | bytes 589832 | tf_op jit(solution)/shard_map/ppermute | solution.py:30
  51.9 0.1 shard_map.123
  51.9 0.0 collective-permute-done.5.moved.rest_0_
  51.9 0.4 collective-permute-start.4
  52.4 1.0 %shard_map.124 = (f32[128,256]{1,0:T(8,128)S(1)}, f32[128,256]{1,0:T(8,128)S(1)}) custom-call(bf16[128,8192]{1,0:T(8,128)(2,1)S(1)} %copy-done, bf16[128,1536]{1,0:T(8,128)(2,1)S(1)} %collective-permute-done.5.moved.rest_0_, bf16[4096,256]{1,0:T(8,128)(2,1)S(1)} %get-tuple-element.28.weight), custom_call_target="tpu_custom_call" | custom-call | bytes 1048576 | tf_op jit(solution)/shard_map/pallas_call | solution.py:60
  53.4 1.6 %collective-permute-start.10 = (f32[64,256]{1,0:T(8,128)S(1)}, f32[64,256]{1,0:T(8,128)S(1)}, u32[]{:S(2)}, u32[]{:S(2)}) collective-permute-start(f32[64,256]{1,0:T(8,128)S(1)} %shard_map.129.refs_4_), channel_id=1, source_target_pairs={{0,16},{8,24},{16,0},{24,8},{1,17},{9,25},{17,1},{25,9},{2,18},{10... | collective-permute-start | bytes 196616 | tf_op jit(solution)/shard_map/ppermute | solution.py:30
  54.9 0.3 shard_map.127
  55.3 1.6 %collective-permute-start.8 = (bf16[128,256]{1,0:T(8,128)(2,1)S(1)}, bf16[128,256]{1,0:T(8,128)(2,1)S(1)}, u32[]{:S(2)}, u32[]{:S(2)}) collective-permute-start(bf16[128,256]{1,0:T(8,128)(2,1)S(1)} %shard_map.127), channel_id=1, source_target_pairs={{0,4},{4,0},{1,5},{5,1},{2,6},{6,2},{3,7},{7,3},{8,12},{12,8},{9,1... | collective-permute-start | bytes 196616 | tf_op jit(solution)/shard_map/ppermute | solution.py:30
  56.8 3.6 %shard_map.136.rest_1_ = bf16[4096,256]{1,0:T(8,128)(2,1)} custom-call(bf16[128,8192]{1,0:T(8,128)(2,1)S(1)} %copy-done, bf16[128,256]{1,0:T(8,128)(2,1)S(1)} %copy-done.1, bf16[128,256]{1,0:T(8,128)(2,1)S(1)} %collective-permute-done.other.other_cot, bf16[128,1536]{1,0:T(8,128)(2,1)S(1)} %collective-permute-done.5.moved.rest_0_, ...), custom_call_target="tpu_custom_call" | custom-call | flops 402653184 | bytes 1048576 | tf_op jit(solution)/shard_map/pallas_call | solution.py:60
  60.4 1.7 %shard_map.137 = bf16[4096,256]{1,0:T(8,128)(2,1)} custom-call(bf16[128,8192]{1,0:T(8,128)(2,1)S(1)} %copy-done, bf16[128,256]{1,0:T(8,128)(2,1)S(1)} %copy-done.1, bf16[128,256]{1,0:T(8,128)(2,1)S(1)} %collective-permute-done.other.other_cot, bf16[128,1024]{1,0:T(8,128)(2,1)S(1)} %collective-permute-done.7.rest_1_.rest_0_, ...), custom_call_target="tpu_custom_call", output_to_operand_aliasing={{}: (4, {})} | custom-call | flops 134217728 | bytes 1048576 | tf_op jit(solution)/shard_map/pallas_call | solution.py:60
  62.1 0.8 %shard_map.134.refs_6_ = bf16[128,2048]{1,0:T(8,128)(2,1)} custom-call(bf16[128,768]{1,0:T(8,128)(2,1)S(1)} %get-tuple-element.40.refs_0_, bf16[128,768]{1,0:T(8,128)(2,1)S(1)} %collective-permute-done.14.refs_1_, bf16[128,768]{1,0:T(8,128)(2,1)S(1)} %get-tuple-element.45.refs_2_, bf16[128,768]{1,0:T(8,128)(2,1)S(1)} %collective-permute-done.18.refs_3_), custom_call_target="tpu_custom_call" | custom-call | bytes 1048576 | tf_op jit(solution)/shard_map/pallas_call | solution.py:60
  63.0 1.3 %shard_map.135 = (bf16[128,2048]{1,0:T(8,128)(2,1)}, bf16[128,256]{1,0:T(8,128)(2,1)}, bf16[32,256]{1,0:T(8,128)(2,1)}, f32[8,256]{1,0:T(8,128)}) custom-call(bf16[128,512]{1,0:T(8,128)(2,1)S(1)} %get-tuple-element.32.refs_0_, bf16[128,512]{1,0:T(8,128)(2,1)S(1)} %collective-permute-done.4.refs_1_, ...), custom_call_target="tpu_custom_call", output_to_operand_aliasing={{0}: (6, {})} | custom-call | bytes 1048576 | tf_op jit(solution)/shard_map/pallas_call | solution.py:60
  (21 shorter events, 0.2 us)
Async XLA Ops:
  0.6 5.5 %collective-permute-start = (bf16[128,256]{1,0:T(8,128)(2,1)}, bf16[128,256]{1,0:T(8,128)(2,1)S(1)}, u32[]{:S(2)}, u32[]{:S(2)}) collective-permute-start(bf16[128,256]{1,0:T(8,128)(2,1)} %own_cot.3), channel_id=1, source_target_pairs={{0,4},{4,0},{1,5},{5,1},{2,6},{6,2},{3,7},{7,3},{8,12},{12,8},{9,1... | collective-permute-start | bytes 196616 | tf_op jit(solution)/shard_map/ppermute | solution.py:30
  3.7 2.5 %copy-start.1 = (bf16[128,256]{1,0:T(8,128)(2,1)S(1)}, bf16[128,256]{1,0:T(8,128)(2,1)}, u32[]{:S(2)}) copy-start(bf16[128,256]{1,0:T(8,128)(2,1)} %own_cot.3) | copy-start | bytes 196612
  5.4 6.4 %copy-start.2 = (f32[40,8,256]{2,1,0:T(8,128)S(1)}, f32[40,8,256]{2,1,0:T(8,128)}, u32[]{:S(2)}) copy-start(f32[40,8,256]{2,1,0:T(8,128)} %params.1) | copy-start | bytes 983044
  5.5 6.4 %copy-start.3 = (f32[40,8,256]{2,1,0:T(8,128)S(1)}, f32[40,8,256]{2,1,0:T(8,128)}, u32[]{:S(2)}) copy-start(f32[40,8,256]{2,1,0:T(8,128)} %moment.1) | copy-start | bytes 983044
  5.5 6.4 %copy-start.4 = (f32[1,32,256]{2,1,0:T(8,128)S(1)}, f32[1,32,256]{2,1,0:T(8,128)}, u32[]{:S(2)}) copy-start(f32[1,32,256]{2,1,0:T(8,128)} %param.11) | copy-start | bytes 98308
  5.5 6.4 %copy-start.5 = (s32[4]{0:T(128)S(1)}, s32[4]{0:T(128)}, u32[]{:S(2)}) copy-start(s32[4]{0:T(128)} %counts.1) | copy-start | bytes 52
  6.9 7.9 %collective-permute-start.16 = (bf16[128,768]{1,0:T(8,128)(2,1)S(1)}, bf16[128,768]{1,0:T(8,128)(2,1)S(1)}, u32[]{:S(2)}, u32[]{:S(2)}) collective-permute-start(bf16[128,768]{1,0:T(8,128)(2,1)S(1)} %get-tuple-element.44), channel_id=1, source_target_pairs={{0,1},{1,0},{2,3},{3,2},{4,5},{5,4},{6,7},{7,6},{8,9},{9,8},{10,11... | collective-permute-start | bytes 589832 | tf_op jit(solution)/shard_map/ppermute | solution.py:30
  9.1 10.0 %collective-permute-start.12 = (bf16[128,768]{1,0:T(8,128)(2,1)S(1)}, bf16[128,768]{1,0:T(8,128)(2,1)S(1)}, u32[]{:S(2)}, u32[]{:S(2)}) collective-permute-start(bf16[128,768]{1,0:T(8,128)(2,1)S(1)} %get-tuple-element.39), channel_id=1, source_target_pairs={{0,1},{1,0},{2,3},{3,2},{4,5},{5,4},{6,7},{7,6},{8,9},{9,8},{10,11... | collective-permute-start | bytes 589832 | tf_op jit(solution)/shard_map/ppermute | solution.py:30
  9.2 12.7 %collective-permute-start.2 = (bf16[128,512]{1,0:T(8,128)(2,1)S(1)}, bf16[128,512]{1,0:T(8,128)(2,1)S(1)}, u32[]{:S(2)}, u32[]{:S(2)}) collective-permute-start(bf16[128,512]{1,0:T(8,128)(2,1)S(1)} %get-tuple-element.31), channel_id=1, source_target_pairs={{0,1},{1,0},{2,3},{3,2},{4,5},{5,4},{6,7},{7,6},{8,9},{9,8},{10,11... | collective-permute-start | bytes 393224 | tf_op jit(solution)/shard_map/ppermute | solution.py:30
  11.1 15.0 %collective-permute-start.15 = (bf16[128,768]{1,0:T(8,128)(2,1)S(1)}, bf16[128,768]{1,0:T(8,128)(2,1)S(1)}, u32[]{:S(2)}, u32[]{:S(2)}) collective-permute-start(bf16[128,768]{1,0:T(8,128)(2,1)S(1)} %get-tuple-element.43), channel_id=1, source_target_pairs={{0,1},{1,0},{2,3},{3,2},{4,5},{5,4},{6,7},{7,6},{8,9},{9,8},{10,11... | collective-permute-start | bytes 589832 | tf_op jit(solution)/shard_map/ppermute | solution.py:30
  12.5 11.3 %copy-start = (bf16[128,8192]{1,0:T(8,128)(2,1)S(1)}, bf16[128,8192]{1,0:T(8,128)(2,1)}, u32[]{:S(2)}) copy-start(bf16[128,8192]{1,0:T(8,128)(2,1)} %hidden.11) | copy-start | bytes 6291460
  12.5 8.5 %collective-permute-start.9 = (f32[48,256]{1,0:T(8,128)S(1)}, f32[48,256]{1,0:T(8,128)S(1)}, u32[]{:S(2)}, u32[]{:S(2)}) collective-permute-start(f32[48,256]{1,0:T(8,128)S(1)} %shard_map.128.packed), channel_id=1, source_target_pairs={{0,8},{8,0},{16,24},{24,16},{1,9},{9,1},{17,25},{25,17},{2,10},{10... | collective-permute-start | bytes 147464 | tf_op jit(solution)/shard_map/ppermute | solution.py:30
  14.9 13.4 %collective-permute-start.11 = (bf16[128,768]{1,0:T(8,128)(2,1)S(1)}, bf16[128,768]{1,0:T(8,128)(2,1)S(1)}, u32[]{:S(2)}, u32[]{:S(2)}) collective-permute-start(bf16[128,768]{1,0:T(8,128)(2,1)S(1)} %get-tuple-element.38), channel_id=1, source_target_pairs={{0,1},{1,0},{2,3},{3,2},{4,5},{5,4},{6,7},{7,6},{8,9},{9,8},{10,11... | collective-permute-start | bytes 589832 | tf_op jit(solution)/shard_map/ppermute | solution.py:30
  19.1 11.0 %collective-permute-start.17 = (bf16[128,768]{1,0:T(8,128)(2,1)S(1)}, bf16[128,768]{1,0:T(8,128)(2,1)S(1)}, u32[]{:S(2)}, u32[]{:S(2)}) collective-permute-start(bf16[128,768]{1,0:T(8,128)(2,1)S(1)} %shard_map.132), channel_id=1, source_target_pairs={{0,4},{4,0},{1,5},{5,1},{2,6},{6,2},{3,7},{7,3},{8,12},{12,8},{9,1... | collective-permute-start | bytes 589832 | tf_op jit(solution)/shard_map/ppermute | solution.py:30
  21.1 10.6 %collective-permute-start.13 = (bf16[128,768]{1,0:T(8,128)(2,1)S(1)}, bf16[128,768]{1,0:T(8,128)(2,1)S(1)}, u32[]{:S(2)}, u32[]{:S(2)}) collective-permute-start(bf16[128,768]{1,0:T(8,128)(2,1)S(1)} %shard_map.130), channel_id=1, source_target_pairs={{0,4},{4,0},{1,5},{5,1},{2,6},{6,2},{3,7},{7,3},{8,12},{12,8},{9,1... | collective-permute-start | bytes 589832 | tf_op jit(solution)/shard_map/ppermute | solution.py:30
  21.9 30.0 %collective-permute-start.5 = (bf16[128,1536]{1,0:T(8,128)(2,1)S(1)}, bf16[128,1536]{1,0:T(8,128)(2,1)S(1)}, u32[]{:S(2)}, u32[]{:S(2)}) collective-permute-start(bf16[128,1536]{1,0:T(8,128)(2,1)S(1)} %get-tuple-element.34), channel_id=1, source_target_pairs={{0,4},{4,0},{1,5},{5,1},{2,6},{6,2},{3,7},{7,3},{8,12},{12,8},{9,1... | collective-permute-start | bytes 1179656 | tf_op jit(solution)/shard_map/ppermute | solution.py:30
  26.1 28.8 %collective-permute-start.6 = (bf16[128,1536]{1,0:T(8,128)(2,1)S(1)}, bf16[128,1536]{1,0:T(8,128)(2,1)S(1)}, u32[]{:S(2)}, u32[]{:S(2)}) collective-permute-start(bf16[128,1536]{1,0:T(8,128)(2,1)S(1)} %shard_map.125), channel_id=1, source_target_pairs={{0,4},{4,0},{1,5},{5,1},{2,6},{6,2},{3,7},{7,3},{8,12},{12,8},{9,1... | collective-permute-start | bytes 1179656 | tf_op jit(solution)/shard_map/ppermute | solution.py:30
  28.3 5.0 %collective-permute-start.1 = (bf16[128,512]{1,0:T(8,128)(2,1)S(1)}, bf16[128,512]{1,0:T(8,128)(2,1)S(1)}, u32[]{:S(2)}, u32[]{:S(2)}) collective-permute-start(bf16[128,512]{1,0:T(8,128)(2,1)S(1)} %get-tuple-element.30), channel_id=1, source_target_pairs={{0,1},{1,0},{2,3},{3,2},{4,5},{5,4},{6,7},{7,6},{8,9},{9,8},{10,11... | collective-permute-start | bytes 393224 | tf_op jit(solution)/shard_map/ppermute | solution.py:30
  30.1 19.2 %collective-permute-start.3 = (bf16[128,512]{1,0:T(8,128)(2,1)S(1)}, bf16[128,512]{1,0:T(8,128)(2,1)S(1)}, u32[]{:S(2)}, u32[]{:S(2)}) collective-permute-start(bf16[128,512]{1,0:T(8,128)(2,1)S(1)} %shard_map.122), channel_id=1, source_target_pairs={{0,4},{4,0},{1,5},{5,1},{2,6},{6,2},{3,7},{7,3},{8,12},{12,8},{9,1... | collective-permute-start | bytes 393224 | tf_op jit(solution)/shard_map/ppermute | solution.py:30
  31.7 21.6 %collective-permute-start.7 = (bf16[128,1024]{1,0:T(8,128)(2,1)S(1)}, bf16[128,1024]{1,0:T(8,128)(2,1)S(1)}, u32[]{:S(2)}, u32[]{:S(2)}) collective-permute-start(bf16[128,1024]{1,0:T(8,128)(2,1)S(1)} %shard_map.126), channel_id=1, source_target_pairs={{0,4},{4,0},{1,5},{5,1},{2,6},{6,2},{3,7},{7,3},{8,12},{12,8},{9,1... | collective-permute-start | bytes 786440 | tf_op jit(solution)/shard_map/ppermute | solution.py:30
  33.3 28.8 %collective-permute-start.18 = (bf16[128,768]{1,0:T(8,128)(2,1)S(1)}, bf16[128,768]{1,0:T(8,128)(2,1)S(1)}, u32[]{:S(2)}, u32[]{:S(2)}) collective-permute-start(bf16[128,768]{1,0:T(8,128)(2,1)S(1)} %get-tuple-element.46), channel_id=1, source_target_pairs={{0,2},{1,3},{2,0},{3,1},{4,6},{5,7},{6,4},{7,5},{8,10},{9,11},{10,... | collective-permute-start | bytes 589832 | tf_op jit(solution)/shard_map/ppermute | solution.py:30
  49.3 12.9 %collective-permute-start.14 = (bf16[128,768]{1,0:T(8,128)(2,1)S(1)}, bf16[128,768]{1,0:T(8,128)(2,1)S(1)}, u32[]{:S(2)}, u32[]{:S(2)}) collective-permute-start(bf16[128,768]{1,0:T(8,128)(2,1)S(1)} %get-tuple-element.41), channel_id=1, source_target_pairs={{0,2},{1,3},{2,0},{3,1},{4,6},{5,7},{6,4},{7,5},{8,10},{9,11},{10,... | collective-permute-start | bytes 589832 | tf_op jit(solution)/shard_map/ppermute | solution.py:30
  51.9 11.0 %collective-permute-start.4 = (bf16[128,512]{1,0:T(8,128)(2,1)S(1)}, bf16[128,512]{1,0:T(8,128)(2,1)S(1)}, u32[]{:S(2)}, u32[]{:S(2)}) collective-permute-start(bf16[128,512]{1,0:T(8,128)(2,1)S(1)} %get-tuple-element.33), channel_id=1, source_target_pairs={{0,2},{1,3},{2,0},{3,1},{4,6},{5,7},{6,4},{7,5},{8,10},{9,11},{10,... | collective-permute-start | bytes 393224 | tf_op jit(solution)/shard_map/ppermute | solution.py:30
  53.4 9.6 %collective-permute-start.10 = (f32[64,256]{1,0:T(8,128)S(1)}, f32[64,256]{1,0:T(8,128)S(1)}, u32[]{:S(2)}, u32[]{:S(2)}) collective-permute-start(f32[64,256]{1,0:T(8,128)S(1)} %shard_map.129.refs_4_), channel_id=1, source_target_pairs={{0,16},{8,24},{16,0},{24,8},{1,17},{9,25},{17,1},{25,9},{2,18},{10... | collective-permute-start | bytes 196616 | tf_op jit(solution)/shard_map/ppermute | solution.py:30
  55.3 7.7 %collective-permute-start.8 = (bf16[128,256]{1,0:T(8,128)(2,1)S(1)}, bf16[128,256]{1,0:T(8,128)(2,1)S(1)}, u32[]{:S(2)}, u32[]{:S(2)}) collective-permute-start(bf16[128,256]{1,0:T(8,128)(2,1)S(1)} %shard_map.127), channel_id=1, source_target_pairs={{0,4},{4,0},{1,5},{5,1},{2,6},{6,2},{3,7},{7,3},{8,12},{12,8},{9,1... | collective-permute-start | bytes 196616 | tf_op jit(solution)/shard_map/ppermute | solution.py:30

commit v2 on v1

--- a/solution.py
+++ b/solution.py
@@ -10,11 +10,11 @@
 
 outer_rate = 0.7
 momentum_rate = 0.9
-PARTS = (6, 6, 4)
+PARTS = (4, 7, 5)
 LOAD_LIMIT = 50
-GRADS = ((0, 1), (2,))
+GRADS = ((0,), (1, 2))
 FINALS = ((0, 1), (2,))
-PIECES = (3, 3, 2)
+PIECES = (4, 3, 1)
 
 
 def matmul_t(a, b):
@@ -90,14 +90,11 @@
     copy.wait()
 
 
-def sent_kernel(weight, own, other, *outs):
-    block = sum(out.shape[1] for out in outs) // 2
-    offset = (1 - lax.axis_index("tensor") % 2) * block
-    for i, out in enumerate(outs):
-        if i == len(outs) // 2:
-            offset = offset - block
+def sent_kernel(weight, cot, *outs):
+    offset = (1 - lax.axis_index("tensor") % 2) * sum(out.shape[1] for out in outs)
+    for out in outs:
         rows = weight[pl.ds(pl.multiple_of(offset, 128), out.shape[1]), :]
-        out[...] = matmul_t((other if i < len(outs) // 2 else own)[...], rows).astype(out.dtype)
+        out[...] = matmul_t(cot[...], rows).astype(out.dtype)
         offset = offset + out.shape[1]
 
 
@@ -321,11 +318,16 @@
     count, flops = len(chunks), 4 * tok_rows * head_cols * block
     part = [jax.ShapeDtypeStruct((tok_rows, chunk), jnp.bfloat16) for chunk in chunks]
     both = [jax.ShapeDtypeStruct((2 * tok_rows, chunk), jnp.float32) for chunk in chunks]
-    inputs = (weight, key_grad, other_cot)
-    gone = call(sent_kernel, part * 2, [VMEM] * 3, [VMEM] * (2 * count), flops=flops)(*inputs)
-    kept = call(kept_kernel, both, [VMEM] * 3, [VMEM] * count, flops=flops)(*inputs)
-    got = [flip(gone[c], "tensor", 1) for c in range(count)]
-    got_own = [flip(gone[count + c], "tensor", 1) for c in range(count)]
+    got_own, got = [
+        [
+            flip(gone, "tensor", 1)
+            for gone in call(sent_kernel, part, [VMEM] * 2, [VMEM] * count, flops=flops)(weight, cot)
+        ]
+        for cot in (key_grad, other_cot)
+    ]
+    kept = call(kept_kernel, both, [VMEM] * 3, [VMEM] * count, flops=flops)(
+        weight, key_grad, other_cot
+    )
     ends = []
     for c in range(count):
         others = call(others_kernel, part[c], [VMEM] * 2, VMEM)(kept[c], got[c])

time: 64.5 us -> 60.4 us (0.936)
  waiting for transfers between devices: 20.4 us -> 15.3 us
  starting transfers between devices: 29.2 us -> 30.1 us
    ppermute x19, waiting for transfers between devices: 20.4 us -> 15.3 us  [flip(): return lax.ppermute(value, axis, [(i, i ^ bit) for i in range(size)])]
    ppermute x19, starting transfers between devices: 29.2 us -> 30.1 us  [flip(): return lax.ppermute(value, axis, [(i, i ^ bit) for i in range(size)])]
    pallas_call x19 -> x20, Pallas kernels: 13.1 us -> 13.2 us  [run(): pl.pallas_call(kernel, out_shape=out_shape, in_specs=in_specs, out_specs=...]
  transfers between devices with their start and end apart: 19 -> 19, of which waited for: 8 -> 7; matrix products, arithmetic and copies ran while one was open for 0% -> 0% of each run, Pallas kernels for 17% -> 19%
where the time goes in v2:
time: 60.4 us; the launch traced here: 60.3 us
  starting transfers between devices  30.1 us (50%)
  waiting for transfers between devices  15.3 us (25%)
  Pallas kernels  13.2 us (22%)
  between operations  1.53 us (3%)
    ppermute x19, starting transfers between devices, flip(): return lax.ppermute(value, axis, [(i, i ^ bit) for i in range(size)])  30.1 us
    ppermute x19, waiting for transfers between devices, flip(): return lax.ppermute(value, axis, [(i, i ^ bit) for i in range(size)])  15.3 us
    pallas_call x20, Pallas kernels, run(): pl.pallas_call(kernel, out_shape=out_shape, in_specs=in_specs, out_specs=...  13.2 us
  transfers between devices with their start and end apart: 19, of which 7 were waited for; matrix products, arithmetic and copies ran while one was open for 0% of the time, Pallas kernels for 19%

profile of v2, /device:TPU:0, one launch (start us, length us, event | category | flops | bytes accessed | tf_op | source)
XLA Modules:
  0.0 60.3 jit_solution(13120273502710793982)
XLA Ops:
  0.6 3.0 %collective-permute-start = (bf16[128,256]{1,0:T(8,128)(2,1)}, bf16[128,256]{1,0:T(8,128)(2,1)S(1)}, u32[]{:S(2)}, u32[]{:S(2)}) collective-permute-start(bf16[128,256]{1,0:T(8,128)(2,1)} %own_cot.3), channel_id=1, source_target_pairs={{0,4},{4,0},{1,5},{5,1},{2,6},{6,2},{3,7},{7,3},{8,12},{12,8},{9,1... | collective-permute-start | bytes 196616 | tf_op jit(solution)/shard_map/ppermute | solution.py:30
  3.7 1.8 %shard_map.119 = (bf16[128,2048]{1,0:T(8,128)(2,1)S(1)}, bf16[4096,256]{1,0:T(8,128)(2,1)S(1)}) custom-call(bf16[128,8192]{1,0:T(8,128)(2,1)} %hidden.11, bf16[4096,256]{1,0:T(8,128)(2,1)} %bitcast.5), custom_call_target="tpu_custom_call" | custom-call | bytes 1048576 | tf_op jit(solution)/shard_map/pallas_call | solution.py:60
  5.5 0.0 copy-start.1
  5.5 0.7 %collective-permute-done.other.cot.other_cot = bf16[128,256]{1,0:T(8,128)(2,1)S(1)} collective-permute-done((bf16[128,256]{1,0:T(8,128)(2,1)}, bf16[128,256]{1,0:T(8,128)(2,1)S(1)}, u32[]{:S(2)}, u32[]{:S(2)}) %collective-permute-start) | collective-permute-done | bytes 65568 | tf_op jit(solution)/shard_map/ppermute | solution.py:30
  6.1 0.5 shard_map.122
  6.6 2.2 %collective-permute-start.16 = (bf16[128,896]{1,0:T(8,128)(2,1)S(1)}, bf16[128,896]{1,0:T(8,128)(2,1)S(1)}, u32[]{:S(2)}, u32[]{:S(2)}) collective-permute-start(bf16[128,896]{1,0:T(8,128)(2,1)S(1)} %get-tuple-element.44), channel_id=1, source_target_pairs={{0,1},{1,0},{2,3},{3,2},{4,5},{5,4},{6,7},{7,6},{8,9},{9,8},{10,11... | collective-permute-start | bytes 688136 | tf_op jit(solution)/shard_map/ppermute | solution.py:30
  8.8 1.5 %collective-permute-start.5 = (bf16[128,2048]{1,0:T(8,128)(2,1)S(1)}, bf16[128,2048]{1,0:T(8,128)(2,1)S(1)}, u32[]{:S(2)}, u32[]{:S(2)}) collective-permute-start(bf16[128,2048]{1,0:T(8,128)(2,1)S(1)} %get-tuple-element.34), channel_id=1, source_target_pairs={{0,4},{4,0},{1,5},{5,1},{2,6},{6,2},{3,7},{7,3},{8,12},{12,8},{9,1... | collective-permute-start | bytes 1572872 | tf_op jit(solution)/shard_map/ppermute | solution.py:30
  10.3 0.4 shard_map.121
  10.7 0.5 collective-permute-start.11
  11.9 0.0 copy-start
  11.9 0.6 %shard_map.129.packed = f32[48,256]{1,0:T(8,128)S(1)} custom-call(s32[1]{0:T(128)S(6)} %copy.17.due_index, s32[4]{0:T(128)S(1)} %copy-done.5, f32[32,256]{1,0:T(8,128)S(1)} %bitcast.3, f32[40,8,256]{2,1,0:T(8,128)S(1)} %copy-done.2, f32[40,8,256]{2,1,0:T(8,128)S(1)} %copy-done.3), custom_call_target="tpu_custom_call" | custom-call | bytes 1048576 | tf_op jit(solution)/shard_map/pallas_call | solution.py:60
  12.6 0.1 collective-permute-start.9
  12.6 1.6 %collective-permute-start.15 = (bf16[128,896]{1,0:T(8,128)(2,1)S(1)}, bf16[128,896]{1,0:T(8,128)(2,1)S(1)}, u32[]{:S(2)}, u32[]{:S(2)}) collective-permute-start(bf16[128,896]{1,0:T(8,128)(2,1)S(1)} %get-tuple-element.43), channel_id=1, source_target_pairs={{0,1},{1,0},{2,3},{3,2},{4,5},{5,4},{6,7},{7,6},{8,9},{9,8},{10,11... | collective-permute-start | bytes 688136 | tf_op jit(solution)/shard_map/ppermute | solution.py:30
  14.3 0.0 collective-permute-done.9.got
  14.3 1.1 %collective-permute-start.12 = (bf16[128,512]{1,0:T(8,128)(2,1)S(1)}, bf16[128,512]{1,0:T(8,128)(2,1)S(1)}, u32[]{:S(2)}, u32[]{:S(2)}) collective-permute-start(bf16[128,512]{1,0:T(8,128)(2,1)S(1)} %get-tuple-element.39), channel_id=1, source_target_pairs={{0,1},{1,0},{2,3},{3,2},{4,5},{5,4},{6,7},{7,6},{8,9},{9,8},{10,11... | collective-permute-start | bytes 393224 | tf_op jit(solution)/shard_map/ppermute | solution.py:30
  15.4 0.0 collective-permute-done.16.got
  15.4 0.9 %collective-permute-start.2 = (bf16[128,640]{1,0:T(8,128)(2,1)S(1)}, bf16[128,640]{1,0:T(8,128)(2,1)S(1)}, u32[]{:S(2)}, u32[]{:S(2)}) collective-permute-start(bf16[128,640]{1,0:T(8,128)(2,1)S(1)} %get-tuple-element.31), channel_id=1, source_target_pairs={{0,1},{1,0},{2,3},{3,2},{4,5},{5,4},{6,7},{7,6},{8,9},{9,8},{10,11... | collective-permute-start | bytes 491528 | tf_op jit(solution)/shard_map/ppermute | solution.py:30
  16.4 0.8 %shard_map.120 = (f32[256,512]{1,0:T(8,128)S(1)}, f32[256,896]{1,0:T(8,128)S(1)}, f32[256,640]{1,0:T(8,128)S(1)}) custom-call(bf16[4096,256]{1,0:T(8,128)(2,1)S(1)} %get-tuple-element.28.weight, bf16[128,256]{1,0:T(8,128)(2,1)S(1)} %copy-done.1, bf16[128,256]{1,0:T(8,128)(2,1)S(1)} %collective-permute-done.other.cot.other_cot), custom_call_target="tpu_custom_call" | custom-call | flops 268435456 | bytes 1048576 | tf_op jit(solution)/shard_map/pallas_call | solution.py:60
  17.2 0.0 collective-permute-done.11.got
  17.2 2.1 %collective-permute-start.17 = (bf16[128,896]{1,0:T(8,128)(2,1)S(1)}, bf16[128,896]{1,0:T(8,128)(2,1)S(1)}, u32[]{:S(2)}, u32[]{:S(2)}) collective-permute-start(bf16[128,896]{1,0:T(8,128)(2,1)S(1)} %shard_map.133), channel_id=1, source_target_pairs={{0,4},{4,0},{1,5},{5,1},{2,6},{6,2},{3,7},{7,3},{8,12},{12,8},{9,1... | collective-permute-start | bytes 688136 | tf_op jit(solution)/shard_map/ppermute | solution.py:30
  19.3 4.7 %collective-permute-done.12.got = bf16[128,512]{1,0:T(8,128)(2,1)S(1)} collective-permute-done((bf16[128,512]{1,0:T(8,128)(2,1)S(1)}, bf16[128,512]{1,0:T(8,128)(2,1)S(1)}, u32[]{:S(2)}, u32[]{:S(2)}) %collective-permute-start.12) | collective-permute-done | bytes 131104 | tf_op jit(solution)/shard_map/ppermute | solution.py:30
  24.1 2.9 %collective-permute-start.6 = (bf16[128,1536]{1,0:T(8,128)(2,1)S(1)}, bf16[128,1536]{1,0:T(8,128)(2,1)S(1)}, u32[]{:S(2)}, u32[]{:S(2)}) collective-permute-start(bf16[128,1536]{1,0:T(8,128)(2,1)S(1)} %shard_map.126), channel_id=1, source_target_pairs={{0,4},{4,0},{1,5},{5,1},{2,6},{6,2},{3,7},{7,3},{8,12},{12,8},{9,1... | collective-permute-start | bytes 1179656 | tf_op jit(solution)/shard_map/ppermute | solution.py:30
  27.0 0.3 collective-permute-done.2.got
  27.3 1.7 %collective-permute-start.1 = (bf16[128,640]{1,0:T(8,128)(2,1)S(1)}, bf16[128,640]{1,0:T(8,128)(2,1)S(1)}, u32[]{:S(2)}, u32[]{:S(2)}) collective-permute-start(bf16[128,640]{1,0:T(8,128)(2,1)S(1)} %get-tuple-element.30), channel_id=1, source_target_pairs={{0,1},{1,0},{2,3},{3,2},{4,5},{5,4},{6,7},{7,6},{8,9},{9,8},{10,11... | collective-permute-start | bytes 491528 | tf_op jit(solution)/shard_map/ppermute | solution.py:30
  29.0 0.0 collective-permute-done.15.got
  29.1 1.6 %collective-permute-start.3 = (bf16[128,640]{1,0:T(8,128)(2,1)S(1)}, bf16[128,640]{1,0:T(8,128)(2,1)S(1)}, u32[]{:S(2)}, u32[]{:S(2)}) collective-permute-start(bf16[128,640]{1,0:T(8,128)(2,1)S(1)} %shard_map.123), channel_id=1, source_target_pairs={{0,4},{4,0},{1,5},{5,1},{2,6},{6,2},{3,7},{7,3},{8,12},{12,8},{9,1... | collective-permute-start | bytes 491528 | tf_op jit(solution)/shard_map/ppermute | solution.py:30
  30.6 0.0 collective-permute-done.17.crossed
  30.6 0.6 collective-permute-start.13
  31.2 0.1 shard_map.134
  31.3 1.8 %collective-permute-done.1.got = bf16[128,640]{1,0:T(8,128)(2,1)S(1)} collective-permute-done((bf16[128,640]{1,0:T(8,128)(2,1)S(1)}, bf16[128,640]{1,0:T(8,128)(2,1)S(1)}, u32[]{:S(2)}, u32[]{:S(2)}) %collective-permute-start.1) | collective-permute-done | bytes 163872 | tf_op jit(solution)/shard_map/ppermute | solution.py:30
  33.2 2.6 %collective-permute-start.18 = (bf16[128,896]{1,0:T(8,128)(2,1)S(1)}, bf16[128,896]{1,0:T(8,128)(2,1)S(1)}, u32[]{:S(2)}, u32[]{:S(2)}) collective-permute-start(bf16[128,896]{1,0:T(8,128)(2,1)S(1)} %get-tuple-element.46), channel_id=1, source_target_pairs={{0,2},{1,3},{2,0},{3,1},{4,6},{5,7},{6,4},{7,5},{8,10},{9,11},{10,... | collective-permute-start | bytes 688136 | tf_op jit(solution)/shard_map/ppermute | solution.py:30
  35.8 4.7 %collective-permute-done.3.crossed = bf16[128,640]{1,0:T(8,128)(2,1)S(1)} collective-permute-done((bf16[128,640]{1,0:T(8,128)(2,1)S(1)}, bf16[128,640]{1,0:T(8,128)(2,1)S(1)}, u32[]{:S(2)}, u32[]{:S(2)}) %collective-permute-start.3) | collective-permute-done | bytes 163872 | tf_op jit(solution)/shard_map/ppermute | solution.py:30
  40.5 1.7 %collective-permute-start.7 = (bf16[128,512]{1,0:T(8,128)(2,1)S(1)}, bf16[128,512]{1,0:T(8,128)(2,1)S(1)}, u32[]{:S(2)}, u32[]{:S(2)}) collective-permute-start(bf16[128,512]{1,0:T(8,128)(2,1)S(1)} %shard_map.127), channel_id=1, source_target_pairs={{0,4},{4,0},{1,5},{5,1},{2,6},{6,2},{3,7},{7,3},{8,12},{12,8},{9,1... | collective-permute-start | bytes 393224 | tf_op jit(solution)/shard_map/ppermute | solution.py:30
  42.2 0.1 shard_map.124
  42.2 0.1 collective-permute-done.13.crossed
  42.3 2.6 %collective-permute-start.4 = (bf16[128,640]{1,0:T(8,128)(2,1)S(1)}, bf16[128,640]{1,0:T(8,128)(2,1)S(1)}, u32[]{:S(2)}, u32[]{:S(2)}) collective-permute-start(bf16[128,640]{1,0:T(8,128)(2,1)S(1)} %get-tuple-element.33), channel_id=1, source_target_pairs={{0,2},{1,3},{2,0},{3,1},{4,6},{5,7},{6,4},{7,5},{8,10},{9,11},{10,... | collective-permute-start | bytes 491528 | tf_op jit(solution)/shard_map/ppermute | solution.py:30
  44.9 0.1 shard_map.132
  45.0 0.0 collective-permute-done.5.moved.rest_0_
  45.0 0.4 collective-permute-start.14
  45.4 1.1 %shard_map.125 = (f32[128,256]{1,0:T(8,128)S(1)}, f32[128,256]{1,0:T(8,128)S(1)}) custom-call(bf16[128,8192]{1,0:T(8,128)(2,1)S(1)} %copy-done, bf16[128,2048]{1,0:T(8,128)(2,1)S(1)} %collective-permute-done.5.moved.rest_0_, bf16[4096,256]{1,0:T(8,128)(2,1)S(1)} %get-tuple-element.28.weight), custom_call_target="tpu_custom_call" | custom-call | bytes 1048576 | tf_op jit(solution)/shard_map/pallas_call | solution.py:60
  46.5 1.6 %collective-permute-start.10 = (f32[64,256]{1,0:T(8,128)S(1)}, f32[64,256]{1,0:T(8,128)S(1)}, u32[]{:S(2)}, u32[]{:S(2)}) collective-permute-start(f32[64,256]{1,0:T(8,128)S(1)} %shard_map.130.refs_4_), channel_id=1, source_target_pairs={{0,16},{8,24},{16,0},{24,8},{1,17},{9,25},{17,1},{25,9},{2,18},{10... | collective-permute-start | bytes 196616 | tf_op jit(solution)/shard_map/ppermute | solution.py:30
  48.0 0.3 shard_map.128
  48.4 1.4 %collective-permute-start.8 = (bf16[128,256]{1,0:T(8,128)(2,1)S(1)}, bf16[128,256]{1,0:T(8,128)(2,1)S(1)}, u32[]{:S(2)}, u32[]{:S(2)}) collective-permute-start(bf16[128,256]{1,0:T(8,128)(2,1)S(1)} %shard_map.128), channel_id=1, source_target_pairs={{0,4},{4,0},{1,5},{5,1},{2,6},{6,2},{3,7},{7,3},{8,12},{12,8},{9,1... | collective-permute-start | bytes 196616 | tf_op jit(solution)/shard_map/ppermute | solution.py:30
  49.7 2.6 %shard_map.137.rest_2_ = bf16[4096,256]{1,0:T(8,128)(2,1)} custom-call(bf16[128,8192]{1,0:T(8,128)(2,1)S(1)} %copy-done, bf16[128,256]{1,0:T(8,128)(2,1)S(1)} %copy-done.1, bf16[128,256]{1,0:T(8,128)(2,1)S(1)} %collective-permute-done.other.cot.other_cot, bf16[128,2048]{1,0:T(8,128)(2,1)S(1)} %collective-permute-done.5.moved.rest_0_), custom_call_target="tpu_custom_call" | custom-call | flops 268435456 | bytes 1048576 | tf_op jit(solution)/shard_map/pallas_call | solution.py:60
  52.4 2.6 %shard_map.138 = bf16[4096,256]{1,0:T(8,128)(2,1)} custom-call(bf16[128,8192]{1,0:T(8,128)(2,1)S(1)} %copy-done, bf16[128,256]{1,0:T(8,128)(2,1)S(1)} %copy-done.1, bf16[128,256]{1,0:T(8,128)(2,1)S(1)} %collective-permute-done.other.cot.other_cot, bf16[128,1536]{1,0:T(8,128)(2,1)S(1)} %collective-permute-done.6.rest_0_, ...), custom_call_target="tpu_custom_call", output_to_operand_aliasing={{}: (5, {})} | custom-call | flops 268435456 | bytes 1048576 | tf_op jit(solution)/shard_map/pallas_call | solution.py:60
  55.0 3.1 %collective-permute-done.14.refs_1_ = bf16[128,512]{1,0:T(8,128)(2,1)S(1)} collective-permute-done((bf16[128,512]{1,0:T(8,128)(2,1)S(1)}, bf16[128,512]{1,0:T(8,128)(2,1)S(1)}, u32[]{:S(2)}, u32[]{:S(2)}) %collective-permute-start.14) | collective-permute-done | bytes 131104 | tf_op jit(solution)/shard_map/ppermute | solution.py:30
  58.1 0.8 %shard_map.135.refs_6_ = bf16[128,2048]{1,0:T(8,128)(2,1)} custom-call(bf16[128,512]{1,0:T(8,128)(2,1)S(1)} %get-tuple-element.40.refs_0_, bf16[128,512]{1,0:T(8,128)(2,1)S(1)} %collective-permute-done.14.refs_1_, bf16[128,896]{1,0:T(8,128)(2,1)S(1)} %get-tuple-element.45.refs_2_, bf16[128,896]{1,0:T(8,128)(2,1)S(1)} %collective-permute-done.18.refs_3_), custom_call_target="tpu_custom_call" | custom-call | bytes 1048576 | tf_op jit(solution)/shard_map/pallas_call | solution.py:60
  58.9 1.4 %shard_map.136 = (bf16[128,2048]{1,0:T(8,128)(2,1)}, bf16[128,256]{1,0:T(8,128)(2,1)}, bf16[32,256]{1,0:T(8,128)(2,1)}, f32[8,256]{1,0:T(8,128)}) custom-call(bf16[128,640]{1,0:T(8,128)(2,1)S(1)} %get-tuple-element.32.refs_0_, bf16[128,640]{1,0:T(8,128)(2,1)S(1)} %collective-permute-done.4.refs_1_, ...), custom_call_target="tpu_custom_call", output_to_operand_aliasing={{0}: (6, {})} | custom-call | bytes 1048576 | tf_op jit(solution)/shard_map/pallas_call | solution.py:60
  (22 shorter events, 0.2 us)
Async XLA Ops:
  0.6 5.5 %collective-permute-start = (bf16[128,256]{1,0:T(8,128)(2,1)}, bf16[128,256]{1,0:T(8,128)(2,1)S(1)}, u32[]{:S(2)}, u32[]{:S(2)}) collective-permute-start(bf16[128,256]{1,0:T(8,128)(2,1)} %own_cot.3), channel_id=1, source_target_pairs={{0,4},{4,0},{1,5},{5,1},{2,6},{6,2},{3,7},{7,3},{8,12},{12,8},{9,1... | collective-permute-start | bytes 196616 | tf_op jit(solution)/shard_map/ppermute | solution.py:30
  5.5 4.8 %copy-start.1 = (bf16[128,256]{1,0:T(8,128)(2,1)S(1)}, bf16[128,256]{1,0:T(8,128)(2,1)}, u32[]{:S(2)}) copy-start(bf16[128,256]{1,0:T(8,128)(2,1)} %own_cot.3) | copy-start | bytes 196612
  6.1 5.8 %copy-start.2 = (f32[40,8,256]{2,1,0:T(8,128)S(1)}, f32[40,8,256]{2,1,0:T(8,128)}, u32[]{:S(2)}) copy-start(f32[40,8,256]{2,1,0:T(8,128)} %params.1) | copy-start | bytes 983044
  6.1 5.8 %copy-start.3 = (f32[40,8,256]{2,1,0:T(8,128)S(1)}, f32[40,8,256]{2,1,0:T(8,128)}, u32[]{:S(2)}) copy-start(f32[40,8,256]{2,1,0:T(8,128)} %moment.1) | copy-start | bytes 983044
  6.1 5.8 %copy-start.4 = (f32[1,32,256]{2,1,0:T(8,128)S(1)}, f32[1,32,256]{2,1,0:T(8,128)}, u32[]{:S(2)}) copy-start(f32[1,32,256]{2,1,0:T(8,128)} %param.11) | copy-start | bytes 98308
  6.1 5.8 %copy-start.5 = (s32[4]{0:T(128)S(1)}, s32[4]{0:T(128)}, u32[]{:S(2)}) copy-start(s32[4]{0:T(128)} %counts.1) | copy-start | bytes 52
  6.6 8.8 %collective-permute-start.16 = (bf16[128,896]{1,0:T(8,128)(2,1)S(1)}, bf16[128,896]{1,0:T(8,128)(2,1)S(1)}, u32[]{:S(2)}, u32[]{:S(2)}) collective-permute-start(bf16[128,896]{1,0:T(8,128)(2,1)S(1)} %get-tuple-element.44), channel_id=1, source_target_pairs={{0,1},{1,0},{2,3},{3,2},{4,5},{5,4},{6,7},{7,6},{8,9},{9,8},{10,11... | collective-permute-start | bytes 688136 | tf_op jit(solution)/shard_map/ppermute | solution.py:30
  8.8 36.2 %collective-permute-start.5 = (bf16[128,2048]{1,0:T(8,128)(2,1)S(1)}, bf16[128,2048]{1,0:T(8,128)(2,1)S(1)}, u32[]{:S(2)}, u32[]{:S(2)}) collective-permute-start(bf16[128,2048]{1,0:T(8,128)(2,1)S(1)} %get-tuple-element.34), channel_id=1, source_target_pairs={{0,4},{4,0},{1,5},{5,1},{2,6},{6,2},{3,7},{7,3},{8,12},{12,8},{9,1... | collective-permute-start | bytes 1572872 | tf_op jit(solution)/shard_map/ppermute | solution.py:30
  10.7 6.5 %collective-permute-start.11 = (bf16[128,512]{1,0:T(8,128)(2,1)S(1)}, bf16[128,512]{1,0:T(8,128)(2,1)S(1)}, u32[]{:S(2)}, u32[]{:S(2)}) collective-permute-start(bf16[128,512]{1,0:T(8,128)(2,1)S(1)} %get-tuple-element.38), channel_id=1, source_target_pairs={{0,1},{1,0},{2,3},{3,2},{4,5},{5,4},{6,7},{7,6},{8,9},{9,8},{10,11... | collective-permute-start | bytes 393224 | tf_op jit(solution)/shard_map/ppermute | solution.py:30
  11.9 7.4 %copy-start = (bf16[128,8192]{1,0:T(8,128)(2,1)S(1)}, bf16[128,8192]{1,0:T(8,128)(2,1)}, u32[]{:S(2)}) copy-start(bf16[128,8192]{1,0:T(8,128)(2,1)} %hidden.11) | copy-start | bytes 6291460
  12.6 1.7 %collective-permute-start.9 = (f32[48,256]{1,0:T(8,128)S(1)}, f32[48,256]{1,0:T(8,128)S(1)}, u32[]{:S(2)}, u32[]{:S(2)}) collective-permute-start(f32[48,256]{1,0:T(8,128)S(1)} %shard_map.129.packed), channel_id=1, source_target_pairs={{0,8},{8,0},{16,24},{24,16},{1,9},{9,1},{17,25},{25,17},{2,10},{10... | collective-permute-start | bytes 147464 | tf_op jit(solution)/shard_map/ppermute | solution.py:30
  12.6 16.4 %collective-permute-start.15 = (bf16[128,896]{1,0:T(8,128)(2,1)S(1)}, bf16[128,896]{1,0:T(8,128)(2,1)S(1)}, u32[]{:S(2)}, u32[]{:S(2)}) collective-permute-start(bf16[128,896]{1,0:T(8,128)(2,1)S(1)} %get-tuple-element.43), channel_id=1, source_target_pairs={{0,1},{1,0},{2,3},{3,2},{4,5},{5,4},{6,7},{7,6},{8,9},{9,8},{10,11... | collective-permute-start | bytes 688136 | tf_op jit(solution)/shard_map/ppermute | solution.py:30
  14.3 9.8 %collective-permute-start.12 = (bf16[128,512]{1,0:T(8,128)(2,1)S(1)}, bf16[128,512]{1,0:T(8,128)(2,1)S(1)}, u32[]{:S(2)}, u32[]{:S(2)}) collective-permute-start(bf16[128,512]{1,0:T(8,128)(2,1)S(1)} %get-tuple-element.39), channel_id=1, source_target_pairs={{0,1},{1,0},{2,3},{3,2},{4,5},{5,4},{6,7},{7,6},{8,9},{9,8},{10,11... | collective-permute-start | bytes 393224 | tf_op jit(solution)/shard_map/ppermute | solution.py:30
  15.4 11.8 %collective-permute-start.2 = (bf16[128,640]{1,0:T(8,128)(2,1)S(1)}, bf16[128,640]{1,0:T(8,128)(2,1)S(1)}, u32[]{:S(2)}, u32[]{:S(2)}) collective-permute-start(bf16[128,640]{1,0:T(8,128)(2,1)S(1)} %get-tuple-element.31), channel_id=1, source_target_pairs={{0,1},{1,0},{2,3},{3,2},{4,5},{5,4},{6,7},{7,6},{8,9},{9,8},{10,11... | collective-permute-start | bytes 491528 | tf_op jit(solution)/shard_map/ppermute | solution.py:30
  17.2 13.4 %collective-permute-start.17 = (bf16[128,896]{1,0:T(8,128)(2,1)S(1)}, bf16[128,896]{1,0:T(8,128)(2,1)S(1)}, u32[]{:S(2)}, u32[]{:S(2)}) collective-permute-start(bf16[128,896]{1,0:T(8,128)(2,1)S(1)} %shard_map.133), channel_id=1, source_target_pairs={{0,4},{4,0},{1,5},{5,1},{2,6},{6,2},{3,7},{7,3},{8,12},{12,8},{9,1... | collective-permute-start | bytes 688136 | tf_op jit(solution)/shard_map/ppermute | solution.py:30
  24.1 24.0 %collective-permute-start.6 = (bf16[128,1536]{1,0:T(8,128)(2,1)S(1)}, bf16[128,1536]{1,0:T(8,128)(2,1)S(1)}, u32[]{:S(2)}, u32[]{:S(2)}) collective-permute-start(bf16[128,1536]{1,0:T(8,128)(2,1)S(1)} %shard_map.126), channel_id=1, source_target_pairs={{0,4},{4,0},{1,5},{5,1},{2,6},{6,2},{3,7},{7,3},{8,12},{12,8},{9,1... | collective-permute-start | bytes 1179656 | tf_op jit(solution)/shard_map/ppermute | solution.py:30
  27.3 5.9 %collective-permute-start.1 = (bf16[128,640]{1,0:T(8,128)(2,1)S(1)}, bf16[128,640]{1,0:T(8,128)(2,1)S(1)}, u32[]{:S(2)}, u32[]{:S(2)}) collective-permute-start(bf16[128,640]{1,0:T(8,128)(2,1)S(1)} %get-tuple-element.30), channel_id=1, source_target_pairs={{0,1},{1,0},{2,3},{3,2},{4,5},{5,4},{6,7},{7,6},{8,9},{9,8},{10,11... | collective-permute-start | bytes 491528 | tf_op jit(solution)/shard_map/ppermute | solution.py:30
  29.1 11.4 %collective-permute-start.3 = (bf16[128,640]{1,0:T(8,128)(2,1)S(1)}, bf16[128,640]{1,0:T(8,128)(2,1)S(1)}, u32[]{:S(2)}, u32[]{:S(2)}) collective-permute-start(bf16[128,640]{1,0:T(8,128)(2,1)S(1)} %shard_map.123), channel_id=1, source_target_pairs={{0,4},{4,0},{1,5},{5,1},{2,6},{6,2},{3,7},{7,3},{8,12},{12,8},{9,1... | collective-permute-start | bytes 491528 | tf_op jit(solution)/shard_map/ppermute | solution.py:30
  30.6 11.7 %collective-permute-start.13 = (bf16[128,512]{1,0:T(8,128)(2,1)S(1)}, bf16[128,512]{1,0:T(8,128)(2,1)S(1)}, u32[]{:S(2)}, u32[]{:S(2)}) collective-permute-start(bf16[128,512]{1,0:T(8,128)(2,1)S(1)} %shard_map.131), channel_id=1, source_target_pairs={{0,4},{4,0},{1,5},{5,1},{2,6},{6,2},{3,7},{7,3},{8,12},{12,8},{9,1... | collective-permute-start | bytes 393224 | tf_op jit(solution)/shard_map/ppermute | solution.py:30
  33.2 24.9 %collective-permute-start.18 = (bf16[128,896]{1,0:T(8,128)(2,1)S(1)}, bf16[128,896]{1,0:T(8,128)(2,1)S(1)}, u32[]{:S(2)}, u32[]{:S(2)}) collective-permute-start(bf16[128,896]{1,0:T(8,128)(2,1)S(1)} %get-tuple-element.46), channel_id=1, source_target_pairs={{0,2},{1,3},{2,0},{3,1},{4,6},{5,7},{6,4},{7,5},{8,10},{9,11},{10,... | collective-permute-start | bytes 688136 | tf_op jit(solution)/shard_map/ppermute | solution.py:30
  40.5 6.0 %collective-permute-start.7 = (bf16[128,512]{1,0:T(8,128)(2,1)S(1)}, bf16[128,512]{1,0:T(8,128)(2,1)S(1)}, u32[]{:S(2)}, u32[]{:S(2)}) collective-permute-start(bf16[128,512]{1,0:T(8,128)(2,1)S(1)} %shard_map.127), channel_id=1, source_target_pairs={{0,4},{4,0},{1,5},{5,1},{2,6},{6,2},{3,7},{7,3},{8,12},{12,8},{9,1... | collective-permute-start | bytes 393224 | tf_op jit(solution)/shard_map/ppermute | solution.py:30
  42.3 16.6 %collective-permute-start.4 = (bf16[128,640]{1,0:T(8,128)(2,1)S(1)}, bf16[128,640]{1,0:T(8,128)(2,1)S(1)}, u32[]{:S(2)}, u32[]{:S(2)}) collective-permute-start(bf16[128,640]{1,0:T(8,128)(2,1)S(1)} %get-tuple-element.33), channel_id=1, source_target_pairs={{0,2},{1,3},{2,0},{3,1},{4,6},{5,7},{6,4},{7,5},{8,10},{9,11},{10,... | collective-permute-start | bytes 491528 | tf_op jit(solution)/shard_map/ppermute | solution.py:30
  45.0 13.1 %collective-permute-start.14 = (bf16[128,512]{1,0:T(8,128)(2,1)S(1)}, bf16[128,512]{1,0:T(8,128)(2,1)S(1)}, u32[]{:S(2)}, u32[]{:S(2)}) collective-permute-start(bf16[128,512]{1,0:T(8,128)(2,1)S(1)} %get-tuple-element.41), channel_id=1, source_target_pairs={{0,2},{1,3},{2,0},{3,1},{4,6},{5,7},{6,4},{7,5},{8,10},{9,11},{10,... | collective-permute-start | bytes 393224 | tf_op jit(solution)/shard_map/ppermute | solution.py:30
  46.5 12.4 %collective-permute-start.10 = (f32[64,256]{1,0:T(8,128)S(1)}, f32[64,256]{1,0:T(8,128)S(1)}, u32[]{:S(2)}, u32[]{:S(2)}) collective-permute-start(f32[64,256]{1,0:T(8,128)S(1)} %shard_map.130.refs_4_), channel_id=1, source_target_pairs={{0,16},{8,24},{16,0},{24,8},{1,17},{9,25},{17,1},{25,9},{2,18},{10... | collective-permute-start | bytes 196616 | tf_op jit(solution)/shard_map/ppermute | solution.py:30
  48.4 10.5 %collective-permute-start.8 = (bf16[128,256]{1,0:T(8,128)(2,1)S(1)}, bf16[128,256]{1,0:T(8,128)(2,1)S(1)}, u32[]{:S(2)}, u32[]{:S(2)}) collective-permute-start(bf16[128,256]{1,0:T(8,128)(2,1)S(1)} %shard_map.128), channel_id=1, source_target_pairs={{0,4},{4,0},{1,5},{5,1},{2,6},{6,2},{3,7},{7,3},{8,12},{12,8},{9,1... | collective-permute-start | bytes 196616 | tf_op jit(solution)/shard_map/ppermute | solution.py:30

commit v3 on v2

--- a/solution.py
+++ b/solution.py
@@ -10,11 +10,11 @@
 
 outer_rate = 0.7
 momentum_rate = 0.9
-PARTS = (4, 7, 5)
+PARTS = (5, 7, 4)
 LOAD_LIMIT = 50
-GRADS = ((0,), (1, 2))
+GRADS = ((0,), (1,))
 FINALS = ((0, 1), (2,))
-PIECES = (4, 3, 1)
+PIECES = (4, 4)
 
 
 def matmul_t(a, b):
@@ -144,11 +144,12 @@
 
 
 def last_kernel(base, count, *refs):
-    parts, (own_part, back, packed, got) = refs[: 2 * count], refs[2 * count : 2 * count + 4]
-    out, keys, params_out, moment_out, made, sems = refs[-6:]
-    copies = final_parts(base, parts, out, made, sems)
-    keys[...] = (own_part[...] + back[...].astype(jnp.float32)).astype(keys.dtype)
-    outer_last(params_out.shape[0], moment_out.shape[0], packed, got, params_out, moment_out)
+    parts, (own_part, back) = refs[: 2 * count], refs[2 * count : 2 * count + 2]
+    out, keys, made, sems, keys_made, keys_sem = refs[-6:]
+    keys_made[...] = (own_part[...] + back[...].astype(jnp.float32)).astype(keys.dtype)
+    copies = [pltpu.make_async_copy(keys_made, keys, keys_sem)]
+    copies[0].start()
+    copies += final_parts(base, parts, out, made, sems)
     for copy in copies:
         copy.wait()
 
@@ -178,7 +179,7 @@
 def weight_rows(hidden, moved, own_cot, other_cot, rows, base, before):
     tokens, head_cols = own_cot.shape
     columns = sum(piece.shape[1] for piece in moved)
-    width = math.gcd(512, *(piece.shape[1] for piece in moved))
+    width = math.gcd(1024, *(piece.shape[1] for piece in moved))
     blocks = columns // width
     kept = () if before is None else (before,)
     run = call(
@@ -250,7 +251,7 @@
     out[rows + held :] = jnp.where(here, got[rows:], packed[rows:])
 
 
-def outer_last(rows, own, packed, got, params_out, moment_out):
+def outer_last_kernel(rows, own, packed, got, params_out, moment_out):
     average = packed[:rows] + got[:rows]
     owners = rows // own
     here = lower_half(2, (2 * own, packed.shape[1]))
@@ -289,7 +290,8 @@
         jax.ShapeDtypeStruct((rows, columns), jnp.bfloat16),
         jax.ShapeDtypeStruct((own, columns), jnp.float32),
     )
-    return packed, got, outs
+    kernel = functools.partial(outer_last_kernel, rows, own)
+    return call(kernel, outs, [VMEM, VMEM], (VMEM, VMEM))(packed, got)
 
 
 def on_device(
@@ -356,7 +358,7 @@
             hidden, pieces, key_grad, other_cot, shard_rows, bases[group[0]], weight_grad
         )
 
-    outer, outer_got, outer_outs = outer_step(
+    fresh_params, fresh_moment = outer_step(
         pseudo_grads, outer_params, outer_moment, token_counts, due_index
     )
 
@@ -366,23 +368,24 @@
         before = () if hidden_grad is None else (hidden_grad,)
         parts = [array for c in group for array in ends[c]]
         width = sum(chunks[c] for c in group)
-        extra = (own_part, back, outer, outer_got) if ending else ()
+        extra = (own_part, back) if ending else ()
         outs = (jax.ShapeDtypeStruct((tok_rows, block), jnp.bfloat16),)
-        kernel = functools.partial(final_kernel, base, len(group))
+        kernel, room = functools.partial(final_kernel, base, len(group)), []
         if ending:
-            outs += (part, *outer_outs)
+            outs += (part,)
+            room = [pltpu.VMEM(part.shape, part.dtype), pltpu.SemaphoreType.DMA]
             kernel = functools.partial(last_kernel, base, len(group))
         run = call(
             kernel,
             outs,
             [VMEM] * (len(parts) + len(extra)) + [HBM] * len(before),
-            (HBM,) + (VMEM,) * (len(outs) - 1),
-            [pltpu.VMEM((tok_rows, width), jnp.bfloat16), pltpu.SemaphoreType.DMA((len(group),))],
+            (HBM,) * len(outs),
+            [pltpu.VMEM((tok_rows, width), jnp.bfloat16), pltpu.SemaphoreType.DMA((len(group),))] + room,
             {len(parts) + len(extra): 0} if before else {},
         )
         hidden_grad, *others = run(*parts, *extra, *before)
         base += width
-    keys, fresh_params, fresh_moment = others
+    keys = others[0]
     return (keys, weight_grad[None], hidden_grad, fresh_params, fresh_moment)
 
 

time: 60.4 us -> 66.7 us (1.10)
  waiting for transfers between devices: 15.3 us -> 25.8 us
  starting transfers between devices: 30.1 us -> 26.5 us
  Pallas kernels: 13.2 us -> 12.5 us
    ppermute x19 -> x18, waiting for transfers between devices: 15.3 us -> 25.8 us  [flip(): return lax.ppermute(value, axis, [(i, i ^ bit) for i in range(size)])]
    ppermute x19 -> x18, starting transfers between devices: 30.1 us -> 26.5 us  [flip(): return lax.ppermute(value, axis, [(i, i ^ bit) for i in range(size)])]
    pallas_call x20, Pallas kernels: 13.2 us -> 12.5 us  [run(): pl.pallas_call(kernel, out_shape=out_shape, in_specs=in_specs, out_specs=...]
  transfers between devices with their start and end apart: 19 -> 18, of which waited for: 7 -> 7; matrix products, arithmetic and copies ran while one was open for 0% -> 0% of each run, Pallas kernels for 19% -> 17%
where the time goes in v3:
time: 66.7 us; the launch traced here: 66.5 us
  starting transfers between devices  26.5 us (40%)
  waiting for transfers between devices  25.8 us (39%)
  Pallas kernels  12.5 us (19%)
  between operations  1.55 us (2%)
    ppermute x18, starting transfers between devices, flip(): return lax.ppermute(value, axis, [(i, i ^ bit) for i in range(size)])  26.5 us
    ppermute x18, waiting for transfers between devices, flip(): return lax.ppermute(value, axis, [(i, i ^ bit) for i in range(size)])  25.8 us
    pallas_call x20, Pallas kernels, run(): pl.pallas_call(kernel, out_shape=out_shape, in_specs=in_specs, out_specs=...  12.5 us
  transfers between devices with their start and end apart: 18, of which 7 were waited for; matrix products, arithmetic and copies ran while one was open for 0% of the time, Pallas kernels for 17%

profile of v3, /device:TPU:0, one launch (start us, length us, event | category | flops | bytes accessed | tf_op | source)
XLA Modules:
  0.0 66.5 jit_solution(3844674018103271320)
XLA Ops:
  0.6 3.0 %collective-permute-start = (bf16[128,256]{1,0:T(8,128)(2,1)}, bf16[128,256]{1,0:T(8,128)(2,1)S(1)}, u32[]{:S(2)}, u32[]{:S(2)}) collective-permute-start(bf16[128,256]{1,0:T(8,128)(2,1)} %own_cot.3), channel_id=1, source_target_pairs={{0,4},{4,0},{1,5},{5,1},{2,6},{6,2},{3,7},{7,3},{8,12},{12,8},{9,1... | collective-permute-start | bytes 196616 | tf_op jit(solution)/shard_map/ppermute | solution.py:30
  3.7 1.8 %shard_map.119 = (bf16[128,2048]{1,0:T(8,128)(2,1)S(1)}, bf16[4096,256]{1,0:T(8,128)(2,1)S(1)}) custom-call(bf16[128,8192]{1,0:T(8,128)(2,1)} %hidden.9, bf16[4096,256]{1,0:T(8,128)(2,1)} %bitcast.5), custom_call_target="tpu_custom_call" | custom-call | bytes 1048576 | tf_op jit(solution)/shard_map/pallas_call | solution.py:60
  5.5 0.0 copy-start.1
  5.5 0.7 collective-permute-done.other.cot.other_cot
  6.1 0.4 shard_map.122
  6.6 2.2 %collective-permute-start.13 = (bf16[128,896]{1,0:T(8,128)(2,1)S(1)}, bf16[128,896]{1,0:T(8,128)(2,1)S(1)}, u32[]{:S(2)}, u32[]{:S(2)}) collective-permute-start(bf16[128,896]{1,0:T(8,128)(2,1)S(1)} %get-tuple-element.44), channel_id=1, source_target_pairs={{0,1},{1,0},{2,3},{3,2},{4,5},{5,4},{6,7},{7,6},{8,9},{9,8},{10,11... | collective-permute-start | bytes 688136 | tf_op jit(solution)/shard_map/ppermute | solution.py:30
  8.8 0.4 shard_map.121
  9.2 0.1 collective-permute-start.1
  9.3 2.0 %collective-permute-start.2 = (bf16[128,512]{1,0:T(8,128)(2,1)S(1)}, bf16[128,512]{1,0:T(8,128)(2,1)S(1)}, u32[]{:S(2)}, u32[]{:S(2)}) collective-permute-start(bf16[128,512]{1,0:T(8,128)(2,1)S(1)} %get-tuple-element.31), channel_id=1, source_target_pairs={{0,1},{1,0},{2,3},{3,2},{4,5},{5,4},{6,7},{7,6},{8,9},{9,8},{10,11... | collective-permute-start | bytes 393224 | tf_op jit(solution)/shard_map/ppermute | solution.py:30
  11.3 1.5 %collective-permute-start.5 = (bf16[128,2048]{1,0:T(8,128)(2,1)S(1)}, bf16[128,2048]{1,0:T(8,128)(2,1)S(1)}, u32[]{:S(2)}, u32[]{:S(2)}) collective-permute-start(bf16[128,2048]{1,0:T(8,128)(2,1)S(1)} %get-tuple-element.34), channel_id=1, source_target_pairs={{0,4},{4,0},{1,5},{5,1},{2,6},{6,2},{3,7},{7,3},{8,12},{12,8},{9,1... | collective-permute-start | bytes 1572872 | tf_op jit(solution)/shard_map/ppermute | solution.py:30
  12.8 0.6 collective-permute-start.6
  13.4 4.6 %collective-permute-done.1.got = bf16[128,512]{1,0:T(8,128)(2,1)S(1)} collective-permute-done((bf16[128,512]{1,0:T(8,128)(2,1)S(1)}, bf16[128,512]{1,0:T(8,128)(2,1)S(1)}, u32[]{:S(2)}, u32[]{:S(2)}) %collective-permute-start.1) | collective-permute-done | bytes 131104 | tf_op jit(solution)/shard_map/ppermute | solution.py:30
  18.0 2.0 %collective-permute-start.12 = (bf16[128,896]{1,0:T(8,128)(2,1)S(1)}, bf16[128,896]{1,0:T(8,128)(2,1)S(1)}, u32[]{:S(2)}, u32[]{:S(2)}) collective-permute-start(bf16[128,896]{1,0:T(8,128)(2,1)S(1)} %get-tuple-element.43), channel_id=1, source_target_pairs={{0,1},{1,0},{2,3},{3,2},{4,5},{5,4},{6,7},{7,6},{8,9},{9,8},{10,11... | collective-permute-start | bytes 688136 | tf_op jit(solution)/shard_map/ppermute | solution.py:30
  20.0 0.0 collective-permute-done.13.got
  20.0 0.0 collective-permute-start.9
  20.1 0.8 %shard_map.120 = (f32[256,640]{1,0:T(8,128)S(1)}, f32[256,896]{1,0:T(8,128)S(1)}, f32[256,512]{1,0:T(8,128)S(1)}) custom-call(bf16[4096,256]{1,0:T(8,128)(2,1)S(1)} %get-tuple-element.28.weight, bf16[128,256]{1,0:T(8,128)(2,1)S(1)} %copy-done.1, bf16[128,256]{1,0:T(8,128)(2,1)S(1)} %collective-permute-done.other.cot.other_cot), custom_call_target="tpu_custom_call" | custom-call | flops 268435456 | bytes 1048576 | tf_op jit(solution)/shard_map/pallas_call | solution.py:60
  20.8 0.0 copy-start.2
  20.8 0.0 copy-start.3
  20.8 0.0 copy-start.4
  20.9 0.0 copy-start.5
  20.9 2.0 %collective-permute-start.14 = (bf16[128,896]{1,0:T(8,128)(2,1)S(1)}, bf16[128,896]{1,0:T(8,128)(2,1)S(1)}, u32[]{:S(2)}, u32[]{:S(2)}) collective-permute-start(bf16[128,896]{1,0:T(8,128)(2,1)S(1)} %shard_map.130), channel_id=1, source_target_pairs={{0,4},{4,0},{1,5},{5,1},{2,6},{6,2},{3,7},{7,3},{8,12},{12,8},{9,1... | collective-permute-start | bytes 688136 | tf_op jit(solution)/shard_map/ppermute | solution.py:30
  22.9 4.4 %collective-permute-done.9.got = bf16[128,640]{1,0:T(8,128)(2,1)S(1)} collective-permute-done((bf16[128,640]{1,0:T(8,128)(2,1)S(1)}, bf16[128,640]{1,0:T(8,128)(2,1)S(1)}, u32[]{:S(2)}, u32[]{:S(2)}) %collective-permute-start.9) | collective-permute-done | bytes 163872 | tf_op jit(solution)/shard_map/ppermute | solution.py:30
  27.3 2.0 %collective-permute-start.8 = (bf16[128,640]{1,0:T(8,128)(2,1)S(1)}, bf16[128,640]{1,0:T(8,128)(2,1)S(1)}, u32[]{:S(2)}, u32[]{:S(2)}) collective-permute-start(bf16[128,640]{1,0:T(8,128)(2,1)S(1)} %get-tuple-element.38), channel_id=1, source_target_pairs={{0,1},{1,0},{2,3},{3,2},{4,5},{5,4},{6,7},{7,6},{8,9},{9,8},{10,11... | collective-permute-start | bytes 491528 | tf_op jit(solution)/shard_map/ppermute | solution.py:30
  29.4 1.5 %collective-permute-start.10 = (bf16[128,640]{1,0:T(8,128)(2,1)S(1)}, bf16[128,640]{1,0:T(8,128)(2,1)S(1)}, u32[]{:S(2)}, u32[]{:S(2)}) collective-permute-start(bf16[128,640]{1,0:T(8,128)(2,1)S(1)} %shard_map.128), channel_id=1, source_target_pairs={{0,4},{4,0},{1,5},{5,1},{2,6},{6,2},{3,7},{7,3},{8,12},{12,8},{9,1... | collective-permute-start | bytes 491528 | tf_op jit(solution)/shard_map/ppermute | solution.py:30
  30.9 11.3 %collective-permute-done.14.crossed = bf16[128,896]{1,0:T(8,128)(2,1)S(1)} collective-permute-done((bf16[128,896]{1,0:T(8,128)(2,1)S(1)}, bf16[128,896]{1,0:T(8,128)(2,1)S(1)}, u32[]{:S(2)}, u32[]{:S(2)}) %collective-permute-start.14) | collective-permute-done | bytes 229408 | tf_op jit(solution)/shard_map/ppermute | solution.py:30
  42.2 1.5 %collective-permute-start.3 = (bf16[128,512]{1,0:T(8,128)(2,1)S(1)}, bf16[128,512]{1,0:T(8,128)(2,1)S(1)}, u32[]{:S(2)}, u32[]{:S(2)}) collective-permute-start(bf16[128,512]{1,0:T(8,128)(2,1)S(1)} %shard_map.123), channel_id=1, source_target_pairs={{0,4},{4,0},{1,5},{5,1},{2,6},{6,2},{3,7},{7,3},{8,12},{12,8},{9,1... | collective-permute-start | bytes 393224 | tf_op jit(solution)/shard_map/ppermute | solution.py:30
  43.7 0.1 shard_map.131
  43.8 0.0 collective-permute-done.8.got
  43.8 2.7 %collective-permute-start.15 = (bf16[128,896]{1,0:T(8,128)(2,1)S(1)}, bf16[128,896]{1,0:T(8,128)(2,1)S(1)}, u32[]{:S(2)}, u32[]{:S(2)}) collective-permute-start(bf16[128,896]{1,0:T(8,128)(2,1)S(1)} %get-tuple-element.46), channel_id=1, source_target_pairs={{0,2},{1,3},{2,0},{3,1},{4,6},{5,7},{6,4},{7,5},{8,10},{9,11},{10,... | collective-permute-start | bytes 688136 | tf_op jit(solution)/shard_map/ppermute | solution.py:30
  47.2 0.6 shard_map.136.packed
  47.8 0.1 collective-permute-start.16
  47.9 0.1 shard_map.129
  48.0 0.0 collective-permute-done.3.crossed
  48.0 1.8 %collective-permute-start.11 = (bf16[128,640]{1,0:T(8,128)(2,1)S(1)}, bf16[128,640]{1,0:T(8,128)(2,1)S(1)}, u32[]{:S(2)}, u32[]{:S(2)}) collective-permute-start(bf16[128,640]{1,0:T(8,128)(2,1)S(1)} %get-tuple-element.41), channel_id=1, source_target_pairs={{0,2},{1,3},{2,0},{3,1},{4,6},{5,7},{6,4},{7,5},{8,10},{9,11},{10,... | collective-permute-start | bytes 491528 | tf_op jit(solution)/shard_map/ppermute | solution.py:30
  49.8 0.1 shard_map.124
  49.9 1.2 %collective-permute-start.4 = (bf16[128,512]{1,0:T(8,128)(2,1)S(1)}, bf16[128,512]{1,0:T(8,128)(2,1)S(1)}, u32[]{:S(2)}, u32[]{:S(2)}) collective-permute-start(bf16[128,512]{1,0:T(8,128)(2,1)S(1)} %get-tuple-element.33), channel_id=1, source_target_pairs={{0,2},{1,3},{2,0},{3,1},{4,6},{5,7},{6,4},{7,5},{8,10},{9,11},{10,... | collective-permute-start | bytes 393224 | tf_op jit(solution)/shard_map/ppermute | solution.py:30
  51.1 1.6 %collective-permute-start.17 = (f32[64,256]{1,0:T(8,128)S(1)}, f32[64,256]{1,0:T(8,128)S(1)}, u32[]{:S(2)}, u32[]{:S(2)}) collective-permute-start(f32[64,256]{1,0:T(8,128)S(1)} %shard_map.137.packed), channel_id=1, source_target_pairs={{0,16},{8,24},{16,0},{24,8},{1,17},{9,25},{17,1},{25,9},{2,18},{10... | collective-permute-start | bytes 196616 | tf_op jit(solution)/shard_map/ppermute | solution.py:30
  52.7 1.1 %shard_map.125 = (f32[128,256]{1,0:T(8,128)S(1)}, f32[128,256]{1,0:T(8,128)S(1)}) custom-call(bf16[128,8192]{1,0:T(8,128)(2,1)S(1)} %copy-done, bf16[128,2048]{1,0:T(8,128)(2,1)S(1)} %collective-permute-done.5.moved.rest_0_, bf16[4096,256]{1,0:T(8,128)(2,1)S(1)} %get-tuple-element.28.weight), custom_call_target="tpu_custom_call" | custom-call | bytes 1048576 | tf_op jit(solution)/shard_map/pallas_call | solution.py:60
  53.8 0.3 shard_map.127
  54.1 0.7 %collective-permute-start.7 = (bf16[128,256]{1,0:T(8,128)(2,1)S(1)}, bf16[128,256]{1,0:T(8,128)(2,1)S(1)}, u32[]{:S(2)}, u32[]{:S(2)}) collective-permute-start(bf16[128,256]{1,0:T(8,128)(2,1)S(1)} %shard_map.127), channel_id=1, source_target_pairs={{0,4},{4,0},{1,5},{5,1},{2,6},{6,2},{3,7},{7,3},{8,12},{12,8},{9,1... | collective-permute-start | bytes 196616 | tf_op jit(solution)/shard_map/ppermute | solution.py:30
  54.8 0.6 collective-permute-done.17.got
  55.5 0.6 shard_map.138
  56.1 2.3 %shard_map.134.rest_1_ = bf16[4096,256]{1,0:T(8,128)(2,1)} custom-call(bf16[128,8192]{1,0:T(8,128)(2,1)S(1)} %copy-done, bf16[128,256]{1,0:T(8,128)(2,1)S(1)} %copy-done.1, bf16[128,256]{1,0:T(8,128)(2,1)S(1)} %collective-permute-done.other.cot.other_cot, bf16[128,2048]{1,0:T(8,128)(2,1)S(1)} %collective-permute-done.5.moved.rest_0_), custom_call_target="tpu_custom_call" | custom-call | flops 268435456 | bytes 1048576 | tf_op jit(solution)/shard_map/pallas_call | solution.py:60
  58.4 2.3 %shard_map.135 = bf16[4096,256]{1,0:T(8,128)(2,1)} custom-call(bf16[128,8192]{1,0:T(8,128)(2,1)S(1)} %copy-done, bf16[128,256]{1,0:T(8,128)(2,1)S(1)} %copy-done.1, bf16[128,256]{1,0:T(8,128)(2,1)S(1)} %collective-permute-done.other.cot.other_cot, bf16[128,2048]{1,0:T(8,128)(2,1)S(1)} %collective-permute-done.6.rest_0_, ...), custom_call_target="tpu_custom_call", output_to_operand_aliasing={{}: (4, {})} | custom-call | flops 268435456 | bytes 1048576 | tf_op jit(solution)/shard_map/pallas_call | solution.py:60
  60.7 3.4 %collective-permute-done.11.refs_1_ = bf16[128,640]{1,0:T(8,128)(2,1)S(1)} collective-permute-done((bf16[128,640]{1,0:T(8,128)(2,1)S(1)}, bf16[128,640]{1,0:T(8,128)(2,1)S(1)}, u32[]{:S(2)}, u32[]{:S(2)}) %collective-permute-start.11) | collective-permute-done | bytes 163872 | tf_op jit(solution)/shard_map/ppermute | solution.py:30
  64.1 0.8 %shard_map.132.refs_4_ = bf16[128,2048]{1,0:T(8,128)(2,1)} custom-call(bf16[128,640]{1,0:T(8,128)(2,1)S(1)} %get-tuple-element.40.refs_0_, bf16[128,640]{1,0:T(8,128)(2,1)S(1)} %collective-permute-done.11.refs_1_, bf16[128,896]{1,0:T(8,128)(2,1)S(1)} %get-tuple-element.45.refs_2_, bf16[128,896]{1,0:T(8,128)(2,1)S(1)} %collective-permute-done.15.refs_3_), custom_call_target="tpu_custom_call" | custom-call | bytes 1048576 | tf_op jit(solution)/shard_map/pallas_call | solution.py:60
  65.0 0.9 %collective-permute-done.4.refs_1_ = bf16[128,512]{1,0:T(8,128)(2,1)S(1)} collective-permute-done((bf16[128,512]{1,0:T(8,128)(2,1)S(1)}, bf16[128,512]{1,0:T(8,128)(2,1)S(1)}, u32[]{:S(2)}, u32[]{:S(2)}) %collective-permute-start.4) | collective-permute-done | bytes 131104 | tf_op jit(solution)/shard_map/ppermute | solution.py:30
  65.8 0.7 %shard_map.133 = (bf16[128,2048]{1,0:T(8,128)(2,1)}, bf16[128,256]{1,0:T(8,128)(2,1)}) custom-call(bf16[128,512]{1,0:T(8,128)(2,1)S(1)} %get-tuple-element.32.refs_0_, bf16[128,512]{1,0:T(8,128)(2,1)S(1)} %collective-permute-done.4.refs_1_, f32[128,256]{1,0:T(8,128)S(1)} %get-tuple-element.35.refs_2_, ...), custom_call_target="tpu_custom_call", output_to_operand_aliasing={{0}: (4, {})} | custom-call | bytes 1048576 | tf_op jit(solution)/shard_map/pallas_call | solution.py:60
  (20 shorter events, 0.2 us)
Async XLA Ops:
  0.6 5.5 %collective-permute-start = (bf16[128,256]{1,0:T(8,128)(2,1)}, bf16[128,256]{1,0:T(8,128)(2,1)S(1)}, u32[]{:S(2)}, u32[]{:S(2)}) collective-permute-start(bf16[128,256]{1,0:T(8,128)(2,1)} %own_cot.3), channel_id=1, source_target_pairs={{0,4},{4,0},{1,5},{5,1},{2,6},{6,2},{3,7},{7,3},{8,12},{12,8},{9,1... | collective-permute-start | bytes 196616 | tf_op jit(solution)/shard_map/ppermute | solution.py:30
  5.5 3.3 %copy-start.1 = (bf16[128,256]{1,0:T(8,128)(2,1)S(1)}, bf16[128,256]{1,0:T(8,128)(2,1)}, u32[]{:S(2)}) copy-start(bf16[128,256]{1,0:T(8,128)(2,1)} %own_cot.3) | copy-start | bytes 196612
  6.1 6.7 %copy-start = (bf16[128,8192]{1,0:T(8,128)(2,1)S(1)}, bf16[128,8192]{1,0:T(8,128)(2,1)}, u32[]{:S(2)}) copy-start(bf16[128,8192]{1,0:T(8,128)(2,1)} %hidden.9) | copy-start | bytes 6291460
  6.6 13.5 %collective-permute-start.13 = (bf16[128,896]{1,0:T(8,128)(2,1)S(1)}, bf16[128,896]{1,0:T(8,128)(2,1)S(1)}, u32[]{:S(2)}, u32[]{:S(2)}) collective-permute-start(bf16[128,896]{1,0:T(8,128)(2,1)S(1)} %get-tuple-element.44), channel_id=1, source_target_pairs={{0,1},{1,0},{2,3},{3,2},{4,5},{5,4},{6,7},{7,6},{8,9},{9,8},{10,11... | collective-permute-start | bytes 688136 | tf_op jit(solution)/shard_map/ppermute | solution.py:30
  9.2 8.8 %collective-permute-start.1 = (bf16[128,512]{1,0:T(8,128)(2,1)S(1)}, bf16[128,512]{1,0:T(8,128)(2,1)S(1)}, u32[]{:S(2)}, u32[]{:S(2)}) collective-permute-start(bf16[128,512]{1,0:T(8,128)(2,1)S(1)} %get-tuple-element.30), channel_id=1, source_target_pairs={{0,1},{1,0},{2,3},{3,2},{4,5},{5,4},{6,7},{7,6},{8,9},{9,8},{10,11... | collective-permute-start | bytes 393224 | tf_op jit(solution)/shard_map/ppermute | solution.py:30
  9.3 11.6 %collective-permute-start.2 = (bf16[128,512]{1,0:T(8,128)(2,1)S(1)}, bf16[128,512]{1,0:T(8,128)(2,1)S(1)}, u32[]{:S(2)}, u32[]{:S(2)}) collective-permute-start(bf16[128,512]{1,0:T(8,128)(2,1)S(1)} %get-tuple-element.31), channel_id=1, source_target_pairs={{0,1},{1,0},{2,3},{3,2},{4,5},{5,4},{6,7},{7,6},{8,9},{9,8},{10,11... | collective-permute-start | bytes 393224 | tf_op jit(solution)/shard_map/ppermute | solution.py:30
  11.3 39.8 %collective-permute-start.5 = (bf16[128,2048]{1,0:T(8,128)(2,1)S(1)}, bf16[128,2048]{1,0:T(8,128)(2,1)S(1)}, u32[]{:S(2)}, u32[]{:S(2)}) collective-permute-start(bf16[128,2048]{1,0:T(8,128)(2,1)S(1)} %get-tuple-element.34), channel_id=1, source_target_pairs={{0,4},{4,0},{1,5},{5,1},{2,6},{6,2},{3,7},{7,3},{8,12},{12,8},{9,1... | collective-permute-start | bytes 1572872 | tf_op jit(solution)/shard_map/ppermute | solution.py:30
  12.8 40.9 %collective-permute-start.6 = (bf16[128,2048]{1,0:T(8,128)(2,1)S(1)}, bf16[128,2048]{1,0:T(8,128)(2,1)S(1)}, u32[]{:S(2)}, u32[]{:S(2)}) collective-permute-start(bf16[128,2048]{1,0:T(8,128)(2,1)S(1)} %shard_map.126), channel_id=1, source_target_pairs={{0,4},{4,0},{1,5},{5,1},{2,6},{6,2},{3,7},{7,3},{8,12},{12,8},{9,1... | collective-permute-start | bytes 1572872 | tf_op jit(solution)/shard_map/ppermute | solution.py:30
  18.0 11.3 %collective-permute-start.12 = (bf16[128,896]{1,0:T(8,128)(2,1)S(1)}, bf16[128,896]{1,0:T(8,128)(2,1)S(1)}, u32[]{:S(2)}, u32[]{:S(2)}) collective-permute-start(bf16[128,896]{1,0:T(8,128)(2,1)S(1)} %get-tuple-element.43), channel_id=1, source_target_pairs={{0,1},{1,0},{2,3},{3,2},{4,5},{5,4},{6,7},{7,6},{8,9},{9,8},{10,11... | collective-permute-start | bytes 688136 | tf_op jit(solution)/shard_map/ppermute | solution.py:30
  20.0 7.3 %collective-permute-start.9 = (bf16[128,640]{1,0:T(8,128)(2,1)S(1)}, bf16[128,640]{1,0:T(8,128)(2,1)S(1)}, u32[]{:S(2)}, u32[]{:S(2)}) collective-permute-start(bf16[128,640]{1,0:T(8,128)(2,1)S(1)} %get-tuple-element.39), channel_id=1, source_target_pairs={{0,1},{1,0},{2,3},{3,2},{4,5},{5,4},{6,7},{7,6},{8,9},{9,8},{10,11... | collective-permute-start | bytes 491528 | tf_op jit(solution)/shard_map/ppermute | solution.py:30
  20.8 26.3 %copy-start.2 = (f32[40,8,256]{2,1,0:T(8,128)S(1)}, f32[40,8,256]{2,1,0:T(8,128)}, u32[]{:S(2)}) copy-start(f32[40,8,256]{2,1,0:T(8,128)} %params.1) | copy-start | bytes 983044
  20.8 26.3 %copy-start.3 = (f32[40,8,256]{2,1,0:T(8,128)S(1)}, f32[40,8,256]{2,1,0:T(8,128)}, u32[]{:S(2)}) copy-start(f32[40,8,256]{2,1,0:T(8,128)} %moment.1) | copy-start | bytes 983044
  20.8 26.3 %copy-start.4 = (f32[1,32,256]{2,1,0:T(8,128)S(1)}, f32[1,32,256]{2,1,0:T(8,128)}, u32[]{:S(2)}) copy-start(f32[1,32,256]{2,1,0:T(8,128)} %param.11) | copy-start | bytes 98308
  20.9 26.3 %copy-start.5 = (s32[4]{0:T(128)S(1)}, s32[4]{0:T(128)}, u32[]{:S(2)}) copy-start(s32[4]{0:T(128)} %counts.1) | copy-start | bytes 52
  20.9 21.3 %collective-permute-start.14 = (bf16[128,896]{1,0:T(8,128)(2,1)S(1)}, bf16[128,896]{1,0:T(8,128)(2,1)S(1)}, u32[]{:S(2)}, u32[]{:S(2)}) collective-permute-start(bf16[128,896]{1,0:T(8,128)(2,1)S(1)} %shard_map.130), channel_id=1, source_target_pairs={{0,4},{4,0},{1,5},{5,1},{2,6},{6,2},{3,7},{7,3},{8,12},{12,8},{9,1... | collective-permute-start | bytes 688136 | tf_op jit(solution)/shard_map/ppermute | solution.py:30
  27.3 16.5 %collective-permute-start.8 = (bf16[128,640]{1,0:T(8,128)(2,1)S(1)}, bf16[128,640]{1,0:T(8,128)(2,1)S(1)}, u32[]{:S(2)}, u32[]{:S(2)}) collective-permute-start(bf16[128,640]{1,0:T(8,128)(2,1)S(1)} %get-tuple-element.38), channel_id=1, source_target_pairs={{0,1},{1,0},{2,3},{3,2},{4,5},{5,4},{6,7},{7,6},{8,9},{9,8},{10,11... | collective-permute-start | bytes 491528 | tf_op jit(solution)/shard_map/ppermute | solution.py:30
  29.4 18.4 %collective-permute-start.10 = (bf16[128,640]{1,0:T(8,128)(2,1)S(1)}, bf16[128,640]{1,0:T(8,128)(2,1)S(1)}, u32[]{:S(2)}, u32[]{:S(2)}) collective-permute-start(bf16[128,640]{1,0:T(8,128)(2,1)S(1)} %shard_map.128), channel_id=1, source_target_pairs={{0,4},{4,0},{1,5},{5,1},{2,6},{6,2},{3,7},{7,3},{8,12},{12,8},{9,1... | collective-permute-start | bytes 491528 | tf_op jit(solution)/shard_map/ppermute | solution.py:30
  42.2 5.7 %collective-permute-start.3 = (bf16[128,512]{1,0:T(8,128)(2,1)S(1)}, bf16[128,512]{1,0:T(8,128)(2,1)S(1)}, u32[]{:S(2)}, u32[]{:S(2)}) collective-permute-start(bf16[128,512]{1,0:T(8,128)(2,1)S(1)} %shard_map.123), channel_id=1, source_target_pairs={{0,4},{4,0},{1,5},{5,1},{2,6},{6,2},{3,7},{7,3},{8,12},{12,8},{9,1... | collective-permute-start | bytes 393224 | tf_op jit(solution)/shard_map/ppermute | solution.py:30
  43.8 20.3 %collective-permute-start.15 = (bf16[128,896]{1,0:T(8,128)(2,1)S(1)}, bf16[128,896]{1,0:T(8,128)(2,1)S(1)}, u32[]{:S(2)}, u32[]{:S(2)}) collective-permute-start(bf16[128,896]{1,0:T(8,128)(2,1)S(1)} %get-tuple-element.46), channel_id=1, source_target_pairs={{0,2},{1,3},{2,0},{3,1},{4,6},{5,7},{6,4},{7,5},{8,10},{9,11},{10,... | collective-permute-start | bytes 688136 | tf_op jit(solution)/shard_map/ppermute | solution.py:30
  47.8 2.0 %collective-permute-start.16 = (f32[48,256]{1,0:T(8,128)S(1)}, f32[48,256]{1,0:T(8,128)S(1)}, u32[]{:S(2)}, u32[]{:S(2)}) collective-permute-start(f32[48,256]{1,0:T(8,128)S(1)} %shard_map.136.packed), channel_id=1, source_target_pairs={{0,8},{8,0},{16,24},{24,16},{1,9},{9,1},{17,25},{25,17},{2,10},{10... | collective-permute-start | bytes 147464 | tf_op jit(solution)/shard_map/ppermute | solution.py:30
  48.0 16.2 %collective-permute-start.11 = (bf16[128,640]{1,0:T(8,128)(2,1)S(1)}, bf16[128,640]{1,0:T(8,128)(2,1)S(1)}, u32[]{:S(2)}, u32[]{:S(2)}) collective-permute-start(bf16[128,640]{1,0:T(8,128)(2,1)S(1)} %get-tuple-element.41), channel_id=1, source_target_pairs={{0,2},{1,3},{2,0},{3,1},{4,6},{5,7},{6,4},{7,5},{8,10},{9,11},{10,... | collective-permute-start | bytes 491528 | tf_op jit(solution)/shard_map/ppermute | solution.py:30
  49.9 15.9 %collective-permute-start.4 = (bf16[128,512]{1,0:T(8,128)(2,1)S(1)}, bf16[128,512]{1,0:T(8,128)(2,1)S(1)}, u32[]{:S(2)}, u32[]{:S(2)}) collective-permute-start(bf16[128,512]{1,0:T(8,128)(2,1)S(1)} %get-tuple-element.33), channel_id=1, source_target_pairs={{0,2},{1,3},{2,0},{3,1},{4,6},{5,7},{6,4},{7,5},{8,10},{9,11},{10,... | collective-permute-start | bytes 393224 | tf_op jit(solution)/shard_map/ppermute | solution.py:30
  51.1 4.3 %collective-permute-start.17 = (f32[64,256]{1,0:T(8,128)S(1)}, f32[64,256]{1,0:T(8,128)S(1)}, u32[]{:S(2)}, u32[]{:S(2)}) collective-permute-start(f32[64,256]{1,0:T(8,128)S(1)} %shard_map.137.packed), channel_id=1, source_target_pairs={{0,16},{8,24},{16,0},{24,8},{1,17},{9,25},{17,1},{25,9},{2,18},{10... | collective-permute-start | bytes 196616 | tf_op jit(solution)/shard_map/ppermute | solution.py:30
  54.1 11.7 %collective-permute-start.7 = (bf16[128,256]{1,0:T(8,128)(2,1)S(1)}, bf16[128,256]{1,0:T(8,128)(2,1)S(1)}, u32[]{:S(2)}, u32[]{:S(2)}) collective-permute-start(bf16[128,256]{1,0:T(8,128)(2,1)S(1)} %shard_map.127), channel_id=1, source_target_pairs={{0,4},{4,0},{1,5},{5,1},{2,6},{6,2},{3,7},{7,3},{8,12},{12,8},{9,1... | collective-permute-start | bytes 196616 | tf_op jit(solution)/shard_map/ppermute | solution.py:30
